TPU v7x, 256 devices: a whole 4x4x8 slice. The times are simulated.
256 devices in a mesh: obs: 8 (over z_hi, core), gx: 8 (over y, z_lo), gy: 4 (over x).
Axes of the slice: x: 4, y: 4, z: 8 (z_hi: 4, z_lo: 2; z = z_hi * 2 + z_lo), core: 2. Of those that a mesh axis runs over, the one named last changes fastest.
Arguments:
- closing_costates: float32 [2, 32, 64, 64, 128], P(None, 'obs', 'gx', 'gy'), may hold values from -6.5 to 6.5
- saved_pore_load: float32 [3, 64, 64, 128], P(None, 'gx', 'gy', 'obs'), may hold values from -4 to 4
- saved_heat_field: float32 [3, 64, 64, 128], P(None, 'gx', 'gy', 'obs'), may hold values from -2.5 to -0.5
- saved_dilatation: float32 [3, 64, 64, 128], P(None, 'gx', 'gy', 'obs'), may hold values from -2.5 to -0.5
- saved_conductivity: float32 [3, 64, 64, 128], P(None, 'gx', 'gy', 'obs'), may hold values from 2.5 to 5
- data_residual: float32 [3, 32, 128], P(None, 'obs'), may hold values from -8 to 8
- borehole_flat_position: int32 [32], P('obs'), may hold values from 0 to 4095
- probe_multiplier: int32 [32], P('obs'), may hold values from 1 to 4
Outputs:
- adjoint_start: float32 [2, 32, 64, 64, 128], P(None, 'obs', 'gx', 'gy')
- gradient: float32 [64, 64, 128], P('gx', 'gy', 'obs')
All inputs are finite; a program needn't handle non-finite values.
Results may differ from a plain program's by a relative error of at most 0.0003.
Values sent between devices are 32-bit elements; how exact they have to be, the bound alone decides.
A program may use at most 64 MiB of HBM per device.

v0:
```python
import jax
import jax.numpy as jnp
from jax import lax
from jax.sharding import PartitionSpec as P

ITERS = 4
heat_diffusivity = 2.0


def padded_2(value, sides, width):
    for axis, dim in sides:
        count, length = (lax.axis_size(axis), value.shape[dim])
        up = [(i, (i + 1) % count) for i in range(count - 1)]
        down = [(j, i) for i, j in up]
        last = lax.slice_in_dim(value, length - width, length, axis=dim)
        initial = lax.slice_in_dim(value, 0, width, axis=dim)
        before = lax.ppermute(last, axis, up)
        after = lax.ppermute(initial, axis, down)
        value = jnp.concatenate([before, value, after], axis=dim)
    return value


def neighbour_sum(padded):
    centre = padded[..., 1:-1, 1:-1, :]
    widths = [(0, 0)] * (centre.ndim - 1) + [(1, 1)]
    deeper = jnp.pad(centre, widths)
    summed = padded[..., 2:, 1:-1, :] + padded[..., :-2, 1:-1, :]
    summed = summed + padded[..., 1:-1, 2:, :] + padded[..., 1:-1, :-2, :]
    return summed + deeper[..., 2:] + deeper[..., :-2]


def whole_faces(costate_vector):
    return padded_2(costate_vector, (("gx", 2), ("gy", 3)), 1)


def relax_group(costate_vector, rights, coeffs):
    perm_now, coupling, diag_p, heat_main_entry = coeffs
    padded = whole_faces(costate_vector)
    near = neighbour_sum(padded)
    new_p = (rights[0] + perm_now * near[0] + coupling * costate_vector[1]) / diag_p
    new_t = (rights[1] + heat_diffusivity * near[1] + coupling * new_p) / heat_main_entry
    return jnp.stack([new_p, new_t])


def local(
    closing_costates,
    saved_pore_load,
    saved_heat_field,
    saved_dilatation,
    saved_conductivity,
    data_residual,
    borehole_flat_position,
    probe_multiplier,
):
    step_count = saved_pore_load.shape[0]
    cells_x = closing_costates.shape[2]
    cells_y = closing_costates.shape[3]
    full_y = cells_y * lax.axis_size("gy")
    rows_x = lax.axis_index("gx") * cells_x + jnp.arange(cells_x, dtype=jnp.int32)
    cols_y = lax.axis_index("gy") * cells_y + jnp.arange(cells_y, dtype=jnp.int32)
    flat_index = rows_x[:, None] * full_y + cols_y[None, :]
    well_mask = (flat_index[None] == borehole_flat_position[:, None, None]).astype(jnp.float32)[
        ..., None
    ]
    weights = probe_multiplier.astype(jnp.float32)
    costate_vector = closing_costates
    gradient_shard = jnp.zeros(saved_pore_load.shape[1:], jnp.float32)
    for backward_counter in range(step_count - 1, -1, -1):
        pressure_now, present_heat_field, strain_now, perm_now = (
            lax.all_gather(saved_pore_load[backward_counter], "obs", axis=2, tiled=True),
            lax.all_gather(saved_heat_field[backward_counter], "obs", axis=2, tiled=True),
            lax.all_gather(saved_dilatation[backward_counter], "obs", axis=2, tiled=True),
            lax.all_gather(saved_conductivity[backward_counter], "obs", axis=2, tiled=True),
        )
        store_p = jnp.exp(strain_now)
        kept_heat_field = jnp.exp(0.5 * present_heat_field)
        coupling = 0.2 * jnp.tanh(pressure_now)
        diag_p = store_p + 6.0 * perm_now
        heat_main_entry = kept_heat_field + 6.0 * heat_diffusivity
        coeffs = (perm_now, coupling, diag_p, heat_main_entry)
        right_p = (
            store_p * costate_vector[0]
            + well_mask * data_residual[backward_counter][:, None, None, :]
        )
        heat_source_term = kept_heat_field * costate_vector[1]
        rights = jnp.stack([right_p, heat_source_term])
        for sweep_index in range(ITERS):
            costate_vector = relax_group(costate_vector, rights, coeffs)
        padded_p = padded_2(pressure_now, (("gx", 0), ("gy", 1)), 1)
        laplace = neighbour_sum(padded_p) - 6.0 * pressure_now
        weighted = jnp.sum(weights[:, None, None, None] * costate_vector[0], axis=0)
        grad_term = perm_now * laplace * weighted
        gradient_shard = gradient_shard + lax.psum_scatter(
            grad_term, "obs", scatter_dimension=2, tiled=True
        )
    return (costate_vector, gradient_shard)


def solution(mesh):
    return jax.shard_map(
        local,
        mesh=mesh,
        in_specs=(
            P(None, "obs", "gx", "gy", None),
            P(None, "gx", "gy", "obs"),
            P(None, "gx", "gy", "obs"),
            P(None, "gx", "gy", "obs"),
            P(None, "gx", "gy", "obs"),
            P(None, "obs", None),
            P("obs"),
            P("obs"),
        ),
        out_specs=(P(None, "obs", "gx", "gy", None), P("gx", "gy", "obs")),
        check_vma=False,
    )
```

profile of v0, /device:TPU:2, one launch (start us, length us, event | category | flops | bytes accessed | tf_op | source)
XLA Modules:
  0.0 513.5 jit_solution(1496356348282304289)
XLA Ops:
  9.4 4.5 collective-permute-start.1
  14.1 18.6 %all-gather.4 = f32[1,8,16,128]{2,1,0,3:T(8,128)S(1)} all-gather(f32[1,8,16,16]{2,1,0,3:T(8,128)S(1)} %copy.160), channel_id=6, replica_groups=mesh['obs'=8,'gx'=8,'gy'=4] {'obs'}, dimensions={3}, use_global_device_ids=true | all-gather | bytes 73728 | tf_op jit(solution)/shard_map/all_gather | solution.py:70
  34.7 5.5 %collective-permute-start.49 = (f32[1,16,128]{1,2,0:T(8,128)}, f32[1,16,128]{1,2,0:T(8,128)}, u32[]{:S(2)}, u32[]{:S(2)}) collective-permute-start(f32[1,16,128]{1,2,0:T(8,128)} %bitcast.18), channel_id=1, source_target_pairs={{0,4},{4,8},{8,12},{12,16},{16,20},{20,24},{24,28},{1,5},{5,9},{9,... | collective-permute-start | bytes 24584 | tf_op jit(solution)/shard_map/ppermute | solution.py:17
  40.4 15.2 %all-gather.7 = f32[1,8,16,128]{2,1,0,3:T(8,128)S(1)} all-gather(f32[1,8,16,16]{2,1,0,3:T(8,128)S(1)} %copy.163), channel_id=9, replica_groups=mesh['obs'=8,'gx'=8,'gy'=4] {'obs'}, dimensions={3}, use_global_device_ids=true | all-gather | bytes 73728 | tf_op jit(solution)/shard_map/all_gather | solution.py:70
  59.3 15.2 %all-gather.5 = f32[1,8,16,128]{2,1,0,3:T(8,128)S(1)} all-gather(f32[1,8,16,16]{2,1,0,3:T(8,128)S(1)} %copy.161), channel_id=7, replica_groups=mesh['obs'=8,'gx'=8,'gy'=4] {'obs'}, dimensions={3}, use_global_device_ids=true | all-gather | bytes 73728 | tf_op jit(solution)/shard_map/all_gather | solution.py:71
  77.0 15.1 %all-gather.10 = f32[1,8,16,128]{2,1,0,3:T(8,128)S(1)} all-gather(f32[1,8,16,16]{2,1,0,3:T(8,128)S(1)} %copy.166), channel_id=12, replica_groups=mesh['obs'=8,'gx'=8,'gy'=4] {'obs'}, dimensions={3}, use_global_device_ids=true | all-gather | bytes 73728 | tf_op jit(solution)/shard_map/all_gather | solution.py:70
  92.9 15.0 %all-gather.3 = f32[1,8,16,128]{2,1,0,3:T(8,128)S(1)} all-gather(f32[1,8,16,16]{2,1,0,3:T(8,128)S(1)} %copy.159), channel_id=5, replica_groups=mesh['obs'=8,'gx'=8,'gy'=4] {'obs'}, dimensions={3}, use_global_device_ids=true | all-gather | bytes 73728 | tf_op jit(solution)/shard_map/all_gather | solution.py:73
  108.1 15.2 %all-gather.6 = f32[1,8,16,128]{2,1,0,3:T(8,128)S(1)} all-gather(f32[1,8,16,16]{2,1,0,3:T(8,128)S(1)} %copy.162), channel_id=8, replica_groups=mesh['obs'=8,'gx'=8,'gy'=4] {'obs'}, dimensions={3}, use_global_device_ids=true | all-gather | bytes 73728 | tf_op jit(solution)/shard_map/all_gather | solution.py:73
  123.5 15.2 %all-gather.9 = f32[1,8,16,128]{2,1,0,3:T(8,128)S(1)} all-gather(f32[1,8,16,16]{2,1,0,3:T(8,128)S(1)} %copy.165), channel_id=11, replica_groups=mesh['obs'=8,'gx'=8,'gy'=4] {'obs'}, dimensions={3}, use_global_device_ids=true | all-gather | bytes 73728 | tf_op jit(solution)/shard_map/all_gather | solution.py:73
  138.8 15.2 %all-gather.2 = f32[1,8,16,128]{2,1,0,3:T(8,128)S(1)} all-gather(f32[1,8,16,16]{2,1,0,3:T(8,128)S(1)} %copy.158), channel_id=4, replica_groups=mesh['obs'=8,'gx'=8,'gy'=4] {'obs'}, dimensions={3}, use_global_device_ids=true | all-gather | bytes 73728 | tf_op jit(solution)/shard_map/all_gather | solution.py:72
  154.3 15.2 %all-gather.1 = f32[1,8,16,128]{2,1,0,3:T(8,128)S(1)} all-gather(f32[1,8,16,16]{2,1,0,3:T(8,128)S(1)} %copy.157), channel_id=3, replica_groups=mesh['obs'=8,'gx'=8,'gy'=4] {'obs'}, dimensions={3}, use_global_device_ids=true | all-gather | bytes 73728 | tf_op jit(solution)/shard_map/all_gather | solution.py:72
  169.6 15.1 %all-gather = f32[1,8,16,128]{2,1,0,3:T(8,128)S(1)} all-gather(f32[1,8,16,16]{2,1,0,3:T(8,128)S(1)} %copy.156), channel_id=2, replica_groups=mesh['obs'=8,'gx'=8,'gy'=4] {'obs'}, dimensions={3}, use_global_device_ids=true | all-gather | bytes 73728 | tf_op jit(solution)/shard_map/all_gather | solution.py:72
  186.6 2.4 collective-permute-start.2
  189.0 3.4 collective-permute-start.3
  196.1 4.0 collective-permute-start.5
  202.1 15.1 %all-gather.8 = f32[1,8,16,128]{2,1,0,3:T(8,128)S(1)} all-gather(f32[1,8,16,16]{2,1,0,3:T(8,128)S(1)} %copy.164), channel_id=10, replica_groups=mesh['obs'=8,'gx'=8,'gy'=4] {'obs'}, dimensions={3}, use_global_device_ids=true | all-gather | bytes 73728 | tf_op jit(solution)/shard_map/all_gather | solution.py:71
  217.4 1.9 collective-permute-start.6
  219.4 3.9 collective-permute-start.7
  225.9 7.6 %collective-permute-start.9 = (f32[2,4,1,16,128]{4,3,2,1,0:T(8,128)S(1)}, f32[2,4,1,16,128]{4,3,2,1,0:T(8,128)S(1)}, u32[]{:S(2)}, u32[]{:S(2)}) collective-permute-start(f32[2,4,1,16,128]{4,3,2,1,0:T(8,128)S(1)} %get-tuple-element.79), channel_id=1, source_target_pairs={{0,4},{4,8},{8,12},{12,16},{16,20},{20,24},{24,28},{1,5},{5,9},{9,... | collective-permute-start | bytes 196616 | tf_op jit(solution)/shard_map/ppermute | solution.py:17
  235.4 4.9 collective-permute-done.8
  240.4 1.9 collective-permute-start.10
  242.3 3.9 collective-permute-start.11
  246.3 1.9 collective-permute-done.11
  248.9 4.8 collective-permute-start.13
  255.8 4.0 collective-permute-done.12
  259.9 1.9 collective-permute-start.14
  261.8 3.9 collective-permute-start.15
  268.4 3.0 collective-permute-start.17
  273.3 4.3 collective-permute-done.16
  277.7 1.9 collective-permute-start.18
  279.6 3.9 collective-permute-start.19
  287.4 4.5 collective-permute-start.21
  295.4 16.6 %all-gather.11 = f32[1,8,16,128]{2,1,0,3:T(8,128)} all-gather(f32[1,8,16,16]{2,1,0,3:T(8,128)} %copy.167), channel_id=13, replica_groups=mesh['obs'=8,'gx'=8,'gy'=4] {'obs'}, dimensions={3}, use_global_device_ids=true | all-gather | bytes 73728 | tf_op jit(solution)/shard_map/all_gather | solution.py:71
  314.7 1.9 collective-permute-start.22
  316.7 3.9 collective-permute-start.23
  324.6 4.6 collective-permute-start.25
  331.2 4.2 collective-permute-done.24
  335.5 1.9 collective-permute-start.26
  337.4 3.9 collective-permute-start.27
  345.2 2.9 collective-permute-start.29
  351.9 2.4 collective-permute-done.28
  354.3 1.9 collective-permute-start.30
  356.3 3.9 collective-permute-start.31
  363.4 3.2 collective-permute-start.33
  368.5 5.2 %collective-permute-start.53 = (f32[1,16,128]{1,2,0:T(8,128)}, f32[1,16,128]{1,2,0:T(8,128)}, u32[]{:S(2)}, u32[]{:S(2)}) collective-permute-start(f32[1,16,128]{1,2,0:T(8,128)} %bitcast.29), channel_id=1, source_target_pairs={{0,4},{4,8},{8,12},{12,16},{16,20},{20,24},{24,28},{1,5},{5,9},{9,... | collective-permute-start | bytes 24584 | tf_op jit(solution)/shard_map/ppermute | solution.py:17
  376.9 1.9 collective-permute-start.34
  378.8 3.9 collective-permute-start.35
  386.6 4.5 collective-permute-start.37
  393.1 5.3 %collective-permute-start.57 = (f32[1,16,128]{1,2,0:T(8,128)}, f32[1,16,128]{1,2,0:T(8,128)}, u32[]{:S(2)}, u32[]{:S(2)}) collective-permute-start(f32[1,16,128]{1,2,0:T(8,128)} %bitcast.39), channel_id=1, source_target_pairs={{0,4},{4,8},{8,12},{12,16},{16,20},{20,24},{24,28},{1,5},{5,9},{9,... | collective-permute-start | bytes 24584 | tf_op jit(solution)/shard_map/ppermute | solution.py:17
  403.4 1.9 collective-permute-start.38
  405.3 3.9 collective-permute-start.39
  413.1 4.2 collective-permute-start.41
  419.2 3.9 collective-permute-start.51
  424.7 2.5 collective-permute-start.54
  428.7 1.9 collective-permute-start.42
  430.7 3.9 collective-permute-start.43
  437.3 4.7 collective-permute-start.45
  443.9 4.3 collective-permute-done.44
  448.3 2.1 collective-permute-start.46
  450.3 3.9 collective-permute-start.47
  454.3 4.1 collective-permute-start.55
  458.5 2.1 collective-permute-start.58
  462.6 3.9 collective-permute-start.59
  472.1 33.1 %reduce-scatter.4.cloned.1.call-done = f32[16,128]{1,0:T(8,128)} async-done(((f32[128,128]{1,0:T(8,128)}), f32[16,128]{1,0:T(8,128)}) %reduce-scatter.4.cloned.1.call-update) | async-done | bytes 8208
  (424 shorter events, 95.9 us)
Async XLA Ops:
  7.2 498.0 %reduce-scatter.4.cloned.1.call-start = ((), (), s32[]{:S(2)}) async-start(), calls=%async_computation.1 | async-start | bytes 73728
  8.1 178.3 %collective-permute-start = (f32[2,4,1,16,128]{4,3,2,1,0:T(8,128)S(1)}, f32[2,4,1,16,128]{4,3,2,1,0:T(8,128)S(1)}, u32[]{:S(2)}, u32[]{:S(2)}) collective-permute-start(f32[2,4,1,16,128]{4,3,2,1,0:T(8,128)S(1)} %get-tuple-element.83), channel_id=1, source_target_pairs={{4,0},{8,4},{12,8},{16,12},{20,16},{24,20},{28,24},{5,1},{9,5},{13... | collective-permute-start | bytes 196616 | tf_op jit(solution)/shard_map/ppermute | solution.py:18
  9.4 177.0 %collective-permute-start.1 = (f32[2,4,1,16,128]{4,3,2,1,0:T(8,128)S(1)}, f32[2,4,1,16,128]{4,3,2,1,0:T(8,128)S(1)}, u32[]{:S(2)}, u32[]{:S(2)}) collective-permute-start(f32[2,4,1,16,128]{4,3,2,1,0:T(8,128)S(1)} %get-tuple-element.84), channel_id=1, source_target_pairs={{0,4},{4,8},{8,12},{12,16},{16,20},{20,24},{24,28},{1,5},{5,9},{9,... | collective-permute-start | bytes 196616 | tf_op jit(solution)/shard_map/ppermute | solution.py:17
  33.5 335.0 %collective-permute-start.48 = (f32[1,16,128]{1,2,0:T(8,128)}, f32[1,16,128]{1,2,0:T(8,128)}, u32[]{:S(2)}, u32[]{:S(2)}) collective-permute-start(f32[1,16,128]{1,2,0:T(8,128)} %bitcast.17), channel_id=1, source_target_pairs={{4,0},{8,4},{12,8},{16,12},{20,16},{24,20},{28,24},{5,1},{9,5},{13... | collective-permute-start | bytes 24584 | tf_op jit(solution)/shard_map/ppermute | solution.py:18
  34.7 339.8 %collective-permute-start.49 = (f32[1,16,128]{1,2,0:T(8,128)}, f32[1,16,128]{1,2,0:T(8,128)}, u32[]{:S(2)}, u32[]{:S(2)}) collective-permute-start(f32[1,16,128]{1,2,0:T(8,128)} %bitcast.18), channel_id=1, source_target_pairs={{0,4},{4,8},{8,12},{12,16},{16,20},{20,24},{24,28},{1,5},{5,9},{9,... | collective-permute-start | bytes 24584 | tf_op jit(solution)/shard_map/ppermute | solution.py:17
  56.3 336.7 %collective-permute-start.52 = (f32[1,16,128]{1,2,0:T(8,128)}, f32[1,16,128]{1,2,0:T(8,128)}, u32[]{:S(2)}, u32[]{:S(2)}) collective-permute-start(f32[1,16,128]{1,2,0:T(8,128)} %bitcast.28), channel_id=1, source_target_pairs={{4,0},{8,4},{12,8},{16,12},{20,16},{24,20},{28,24},{5,1},{9,5},{13... | collective-permute-start | bytes 24584 | tf_op jit(solution)/shard_map/ppermute | solution.py:18
  74.8 193.4 %copy-start.26 = (f32[8,16,128]{2,1,0:T(8,128)}, f32[8,16,128]{2,1,0:T(8,128)S(1)}, u32[]{:S(2)}) copy-start(f32[8,16,128]{2,1,0:T(8,128)S(1)} %broadcast_add_fusion.2) | copy-start | bytes 196612
  74.8 193.3 %copy-start.28 = (f32[8,16,128]{2,1,0:T(8,128)}, f32[8,16,128]{2,1,0:T(8,128)S(1)}, u32[]{:S(2)}) copy-start(f32[8,16,128]{2,1,0:T(8,128)S(1)} %exponential_bitcast_fusion.2) | copy-start | bytes 196612
  123.5 200.3 %copy-start.15 = (f32[1,8,16,128]{3,2,1,0:T(8,128)}, f32[1,8,16,128]{3,2,1,0:T(8,128)S(1)}, u32[]{:S(2)}) copy-start(f32[1,8,16,128]{3,2,1,0:T(8,128)S(1)} %copy.131) | copy-start | bytes 196612
  186.6 6.5 %collective-permute-start.2 = (f32[2,4,10,1,128]{4,3,2,1,0:T(1,128)S(1)}, f32[2,4,10,1,128]{4,3,2,1,0:T(1,128)S(1)}, u32[]{:S(2)}, u32[]{:S(2)}) collective-permute-start(f32[2,4,10,1,128]{4,3,2,1,0:T(1,128)S(1)} %get-tuple-element.53), channel_id=1, source_target_pairs={{1,0},{2,1},{3,2},{5,4},{6,5},{7,6},{9,8},{10,9},{11,10},{13,12},{... | collective-permute-start | bytes 122888 | tf_op jit(solution)/shard_map/ppermute | solution.py:18
  189.0 5.9 %collective-permute-start.3 = (f32[2,4,10,1,128]{4,3,2,1,0:T(1,128)S(1)}, f32[2,4,10,1,128]{4,3,2,1,0:T(1,128)S(1)}, u32[]{:S(2)}, u32[]{:S(2)}) collective-permute-start(f32[2,4,10,1,128]{4,3,2,1,0:T(1,128)S(1)} %get-tuple-element.54), channel_id=1, source_target_pairs={{0,1},{1,2},{2,3},{4,5},{5,6},{6,7},{8,9},{9,10},{10,11},{12,13},{... | collective-permute-start | bytes 122888 | tf_op jit(solution)/shard_map/ppermute | solution.py:17
  196.1 21.2 %collective-permute-start.5 = (f32[2,4,1,16,128]{4,3,2,1,0:T(8,128)S(1)}, f32[2,4,1,16,128]{4,3,2,1,0:T(8,128)S(1)}, u32[]{:S(2)}, u32[]{:S(2)}) collective-permute-start(f32[2,4,1,16,128]{4,3,2,1,0:T(8,128)S(1)} %get-tuple-element.81), channel_id=1, source_target_pairs={{0,4},{4,8},{8,12},{12,16},{16,20},{20,24},{24,28},{1,5},{5,9},{9,... | collective-permute-start | bytes 196616 | tf_op jit(solution)/shard_map/ppermute | solution.py:17
  200.1 17.3 %collective-permute-start.4 = (f32[2,4,1,16,128]{4,3,2,1,0:T(8,128)S(1)}, f32[2,4,1,16,128]{4,3,2,1,0:T(8,128)S(1)}, u32[]{:S(2)}, u32[]{:S(2)}) collective-permute-start(f32[2,4,1,16,128]{4,3,2,1,0:T(8,128)S(1)} %get-tuple-element.82), channel_id=1, source_target_pairs={{4,0},{8,4},{12,8},{16,12},{20,16},{24,20},{28,24},{5,1},{9,5},{13... | collective-permute-start | bytes 196616 | tf_op jit(solution)/shard_map/ppermute | solution.py:18
  217.4 5.9 %collective-permute-start.6 = (f32[2,4,10,1,128]{4,3,2,1,0:T(1,128)S(1)}, f32[2,4,10,1,128]{4,3,2,1,0:T(1,128)S(1)}, u32[]{:S(2)}, u32[]{:S(2)}) collective-permute-start(f32[2,4,10,1,128]{4,3,2,1,0:T(1,128)S(1)} %get-tuple-element.51), channel_id=1, source_target_pairs={{1,0},{2,1},{3,2},{5,4},{6,5},{7,6},{9,8},{10,9},{11,10},{13,12},{... | collective-permute-start | bytes 122888 | tf_op jit(solution)/shard_map/ppermute | solution.py:18
  219.4 5.9 %collective-permute-start.7 = (f32[2,4,10,1,128]{4,3,2,1,0:T(1,128)S(1)}, f32[2,4,10,1,128]{4,3,2,1,0:T(1,128)S(1)}, u32[]{:S(2)}, u32[]{:S(2)}) collective-permute-start(f32[2,4,10,1,128]{4,3,2,1,0:T(1,128)S(1)} %get-tuple-element.52), channel_id=1, source_target_pairs={{0,1},{1,2},{2,3},{4,5},{5,6},{6,7},{8,9},{9,10},{10,11},{12,13},{... | collective-permute-start | bytes 122888 | tf_op jit(solution)/shard_map/ppermute | solution.py:17
  225.9 9.5 %collective-permute-start.9 = (f32[2,4,1,16,128]{4,3,2,1,0:T(8,128)S(1)}, f32[2,4,1,16,128]{4,3,2,1,0:T(8,128)S(1)}, u32[]{:S(2)}, u32[]{:S(2)}) collective-permute-start(f32[2,4,1,16,128]{4,3,2,1,0:T(8,128)S(1)} %get-tuple-element.79), channel_id=1, source_target_pairs={{0,4},{4,8},{8,12},{12,16},{16,20},{20,24},{24,28},{1,5},{5,9},{9,... | collective-permute-start | bytes 196616 | tf_op jit(solution)/shard_map/ppermute | solution.py:17
  233.5 6.8 %collective-permute-start.8 = (f32[2,4,1,16,128]{4,3,2,1,0:T(8,128)S(1)}, f32[2,4,1,16,128]{4,3,2,1,0:T(8,128)S(1)}, u32[]{:S(2)}, u32[]{:S(2)}) collective-permute-start(f32[2,4,1,16,128]{4,3,2,1,0:T(8,128)S(1)} %get-tuple-element.80), channel_id=1, source_target_pairs={{4,0},{8,4},{12,8},{16,12},{20,16},{24,20},{28,24},{5,1},{9,5},{13... | collective-permute-start | bytes 196616 | tf_op jit(solution)/shard_map/ppermute | solution.py:18
  240.4 5.9 %collective-permute-start.10 = (f32[2,4,10,1,128]{4,3,2,1,0:T(1,128)S(1)}, f32[2,4,10,1,128]{4,3,2,1,0:T(1,128)S(1)}, u32[]{:S(2)}, u32[]{:S(2)}) collective-permute-start(f32[2,4,10,1,128]{4,3,2,1,0:T(1,128)S(1)} %get-tuple-element.49), channel_id=1, source_target_pairs={{1,0},{2,1},{3,2},{5,4},{6,5},{7,6},{9,8},{10,9},{11,10},{13,12},{... | collective-permute-start | bytes 122888 | tf_op jit(solution)/shard_map/ppermute | solution.py:18
  242.3 5.9 %collective-permute-start.11 = (f32[2,4,10,1,128]{4,3,2,1,0:T(1,128)S(1)}, f32[2,4,10,1,128]{4,3,2,1,0:T(1,128)S(1)}, u32[]{:S(2)}, u32[]{:S(2)}) collective-permute-start(f32[2,4,10,1,128]{4,3,2,1,0:T(1,128)S(1)} %get-tuple-element.50), channel_id=1, source_target_pairs={{0,1},{1,2},{2,3},{4,5},{5,6},{6,7},{8,9},{9,10},{10,11},{12,13},{... | collective-permute-start | bytes 122888 | tf_op jit(solution)/shard_map/ppermute | solution.py:17
  248.9 6.9 %collective-permute-start.13 = (f32[2,4,1,16,128]{4,3,2,1,0:T(8,128)S(1)}, f32[2,4,1,16,128]{4,3,2,1,0:T(8,128)S(1)}, u32[]{:S(2)}, u32[]{:S(2)}) collective-permute-start(f32[2,4,1,16,128]{4,3,2,1,0:T(8,128)S(1)} %get-tuple-element.77), channel_id=1, source_target_pairs={{0,4},{4,8},{8,12},{12,16},{16,20},{20,24},{24,28},{1,5},{5,9},{9,... | collective-permute-start | bytes 196616 | tf_op jit(solution)/shard_map/ppermute | solution.py:17
  253.7 6.2 %collective-permute-start.12 = (f32[2,4,1,16,128]{4,3,2,1,0:T(8,128)S(1)}, f32[2,4,1,16,128]{4,3,2,1,0:T(8,128)S(1)}, u32[]{:S(2)}, u32[]{:S(2)}) collective-permute-start(f32[2,4,1,16,128]{4,3,2,1,0:T(8,128)S(1)} %get-tuple-element.78), channel_id=1, source_target_pairs={{4,0},{8,4},{12,8},{16,12},{20,16},{24,20},{28,24},{5,1},{9,5},{13... | collective-permute-start | bytes 196616 | tf_op jit(solution)/shard_map/ppermute | solution.py:18
  259.9 5.9 %collective-permute-start.14 = (f32[2,4,10,1,128]{4,3,2,1,0:T(1,128)S(1)}, f32[2,4,10,1,128]{4,3,2,1,0:T(1,128)S(1)}, u32[]{:S(2)}, u32[]{:S(2)}) collective-permute-start(f32[2,4,10,1,128]{4,3,2,1,0:T(1,128)S(1)} %get-tuple-element.47), channel_id=1, source_target_pairs={{1,0},{2,1},{3,2},{5,4},{6,5},{7,6},{9,8},{10,9},{11,10},{13,12},{... | collective-permute-start | bytes 122888 | tf_op jit(solution)/shard_map/ppermute | solution.py:18
  261.8 5.9 %collective-permute-start.15 = (f32[2,4,10,1,128]{4,3,2,1,0:T(1,128)S(1)}, f32[2,4,10,1,128]{4,3,2,1,0:T(1,128)S(1)}, u32[]{:S(2)}, u32[]{:S(2)}) collective-permute-start(f32[2,4,10,1,128]{4,3,2,1,0:T(1,128)S(1)} %get-tuple-element.48), channel_id=1, source_target_pairs={{0,1},{1,2},{2,3},{4,5},{5,6},{6,7},{8,9},{9,10},{10,11},{12,13},{... | collective-permute-start | bytes 122888 | tf_op jit(solution)/shard_map/ppermute | solution.py:17
  268.4 4.9 collective-permute-start.17
  271.4 6.2 %collective-permute-start.16 = (f32[2,4,1,16,128]{4,3,2,1,0:T(8,128)S(1)}, f32[2,4,1,16,128]{4,3,2,1,0:T(8,128)S(1)}, u32[]{:S(2)}, u32[]{:S(2)}) collective-permute-start(f32[2,4,1,16,128]{4,3,2,1,0:T(8,128)S(1)} %get-tuple-element.76), channel_id=1, source_target_pairs={{4,0},{8,4},{12,8},{16,12},{20,16},{24,20},{28,24},{5,1},{9,5},{13... | collective-permute-start | bytes 196616 | tf_op jit(solution)/shard_map/ppermute | solution.py:18
  277.7 5.9 %collective-permute-start.18 = (f32[2,4,10,1,128]{4,3,2,1,0:T(1,128)S(1)}, f32[2,4,10,1,128]{4,3,2,1,0:T(1,128)S(1)}, u32[]{:S(2)}, u32[]{:S(2)}) collective-permute-start(f32[2,4,10,1,128]{4,3,2,1,0:T(1,128)S(1)} %get-tuple-element.45), channel_id=1, source_target_pairs={{1,0},{2,1},{3,2},{5,4},{6,5},{7,6},{9,8},{10,9},{11,10},{13,12},{... | collective-permute-start | bytes 122888 | tf_op jit(solution)/shard_map/ppermute | solution.py:18
  279.6 5.9 %collective-permute-start.19 = (f32[2,4,10,1,128]{4,3,2,1,0:T(1,128)S(1)}, f32[2,4,10,1,128]{4,3,2,1,0:T(1,128)S(1)}, u32[]{:S(2)}, u32[]{:S(2)}) collective-permute-start(f32[2,4,10,1,128]{4,3,2,1,0:T(1,128)S(1)} %get-tuple-element.46), channel_id=1, source_target_pairs={{0,1},{1,2},{2,3},{4,5},{5,6},{6,7},{8,9},{9,10},{10,11},{12,13},{... | collective-permute-start | bytes 122888 | tf_op jit(solution)/shard_map/ppermute | solution.py:17
  287.4 26.4 %collective-permute-start.21 = (f32[2,4,1,16,128]{4,3,2,1,0:T(8,128)}, f32[2,4,1,16,128]{4,3,2,1,0:T(8,128)}, u32[]{:S(2)}, u32[]{:S(2)}) collective-permute-start(f32[2,4,1,16,128]{4,3,2,1,0:T(8,128)} %get-tuple-element.73), channel_id=1, source_target_pairs={{0,4},{4,8},{8,12},{12,16},{16,20},{20,24},{24,28},{1,5},{5,9},{9,... | collective-permute-start | bytes 196616 | tf_op jit(solution)/shard_map/ppermute | solution.py:17
  291.9 22.0 %collective-permute-start.20 = (f32[2,4,1,16,128]{4,3,2,1,0:T(8,128)}, f32[2,4,1,16,128]{4,3,2,1,0:T(8,128)}, u32[]{:S(2)}, u32[]{:S(2)}) collective-permute-start(f32[2,4,1,16,128]{4,3,2,1,0:T(8,128)} %get-tuple-element.74), channel_id=1, source_target_pairs={{4,0},{8,4},{12,8},{16,12},{20,16},{24,20},{28,24},{5,1},{9,5},{13... | collective-permute-start | bytes 196616 | tf_op jit(solution)/shard_map/ppermute | solution.py:18
  314.7 6.0 %collective-permute-start.22 = (f32[2,4,10,1,128]{4,3,2,1,0:T(1,128)S(1)}, f32[2,4,10,1,128]{4,3,2,1,0:T(1,128)S(1)}, u32[]{:S(2)}, u32[]{:S(2)}) collective-permute-start(f32[2,4,10,1,128]{4,3,2,1,0:T(1,128)S(1)} %get-tuple-element.43), channel_id=1, source_target_pairs={{1,0},{2,1},{3,2},{5,4},{6,5},{7,6},{9,8},{10,9},{11,10},{13,12},{... | collective-permute-start | bytes 122888 | tf_op jit(solution)/shard_map/ppermute | solution.py:18
  316.7 5.9 %collective-permute-start.23 = (f32[2,4,10,1,128]{4,3,2,1,0:T(1,128)S(1)}, f32[2,4,10,1,128]{4,3,2,1,0:T(1,128)S(1)}, u32[]{:S(2)}, u32[]{:S(2)}) collective-permute-start(f32[2,4,10,1,128]{4,3,2,1,0:T(1,128)S(1)} %get-tuple-element.44), channel_id=1, source_target_pairs={{0,1},{1,2},{2,3},{4,5},{5,6},{6,7},{8,9},{9,10},{10,11},{12,13},{... | collective-permute-start | bytes 122888 | tf_op jit(solution)/shard_map/ppermute | solution.py:17
  324.6 6.6 %collective-permute-start.25 = (f32[2,4,1,16,128]{4,3,2,1,0:T(8,128)S(1)}, f32[2,4,1,16,128]{4,3,2,1,0:T(8,128)S(1)}, u32[]{:S(2)}, u32[]{:S(2)}) collective-permute-start(f32[2,4,1,16,128]{4,3,2,1,0:T(8,128)S(1)} %get-tuple-element.71), channel_id=1, source_target_pairs={{0,4},{4,8},{8,12},{12,16},{16,20},{20,24},{24,28},{1,5},{5,9},{9,... | collective-permute-start | bytes 196616 | tf_op jit(solution)/shard_map/ppermute | solution.py:17
  329.3 6.2 %collective-permute-start.24 = (f32[2,4,1,16,128]{4,3,2,1,0:T(8,128)S(1)}, f32[2,4,1,16,128]{4,3,2,1,0:T(8,128)S(1)}, u32[]{:S(2)}, u32[]{:S(2)}) collective-permute-start(f32[2,4,1,16,128]{4,3,2,1,0:T(8,128)S(1)} %get-tuple-element.72), channel_id=1, source_target_pairs={{4,0},{8,4},{12,8},{16,12},{20,16},{24,20},{28,24},{5,1},{9,5},{13... | collective-permute-start | bytes 196616 | tf_op jit(solution)/shard_map/ppermute | solution.py:18
  335.5 5.9 %collective-permute-start.26 = (f32[2,4,10,1,128]{4,3,2,1,0:T(1,128)S(1)}, f32[2,4,10,1,128]{4,3,2,1,0:T(1,128)S(1)}, u32[]{:S(2)}, u32[]{:S(2)}) collective-permute-start(f32[2,4,10,1,128]{4,3,2,1,0:T(1,128)S(1)} %get-tuple-element.41), channel_id=1, source_target_pairs={{1,0},{2,1},{3,2},{5,4},{6,5},{7,6},{9,8},{10,9},{11,10},{13,12},{... | collective-permute-start | bytes 122888 | tf_op jit(solution)/shard_map/ppermute | solution.py:18
  337.4 5.9 %collective-permute-start.27 = (f32[2,4,10,1,128]{4,3,2,1,0:T(1,128)S(1)}, f32[2,4,10,1,128]{4,3,2,1,0:T(1,128)S(1)}, u32[]{:S(2)}, u32[]{:S(2)}) collective-permute-start(f32[2,4,10,1,128]{4,3,2,1,0:T(1,128)S(1)} %get-tuple-element.42), channel_id=1, source_target_pairs={{0,1},{1,2},{2,3},{4,5},{5,6},{6,7},{8,9},{9,10},{10,11},{12,13},{... | collective-permute-start | bytes 122888 | tf_op jit(solution)/shard_map/ppermute | solution.py:17
  345.2 6.7 %collective-permute-start.29 = (f32[2,4,1,16,128]{4,3,2,1,0:T(8,128)}, f32[2,4,1,16,128]{4,3,2,1,0:T(8,128)S(1)}, u32[]{:S(2)}, u32[]{:S(2)}) collective-permute-start(f32[2,4,1,16,128]{4,3,2,1,0:T(8,128)} %get-tuple-element.69), channel_id=1, source_target_pairs={{0,4},{4,8},{8,12},{12,16},{16,20},{20,24},{24,28},{1,5},{5,9},{9,... | collective-permute-start | bytes 196616 | tf_op jit(solution)/shard_map/ppermute | solution.py:17
  348.1 6.2 %collective-permute-start.28 = (f32[2,4,1,16,128]{4,3,2,1,0:T(8,128)S(1)}, f32[2,4,1,16,128]{4,3,2,1,0:T(8,128)S(1)}, u32[]{:S(2)}, u32[]{:S(2)}) collective-permute-start(f32[2,4,1,16,128]{4,3,2,1,0:T(8,128)S(1)} %get-tuple-element.70), channel_id=1, source_target_pairs={{4,0},{8,4},{12,8},{16,12},{20,16},{24,20},{28,24},{5,1},{9,5},{13... | collective-permute-start | bytes 196616 | tf_op jit(solution)/shard_map/ppermute | solution.py:18
  354.3 6.0 %collective-permute-start.30 = (f32[2,4,10,1,128]{4,3,2,1,0:T(1,128)S(1)}, f32[2,4,10,1,128]{4,3,2,1,0:T(1,128)S(1)}, u32[]{:S(2)}, u32[]{:S(2)}) collective-permute-start(f32[2,4,10,1,128]{4,3,2,1,0:T(1,128)S(1)} %get-tuple-element.39), channel_id=1, source_target_pairs={{1,0},{2,1},{3,2},{5,4},{6,5},{7,6},{9,8},{10,9},{11,10},{13,12},{... | collective-permute-start | bytes 122888 | tf_op jit(solution)/shard_map/ppermute | solution.py:18
  356.3 5.9 %collective-permute-start.31 = (f32[2,4,10,1,128]{4,3,2,1,0:T(1,128)S(1)}, f32[2,4,10,1,128]{4,3,2,1,0:T(1,128)S(1)}, u32[]{:S(2)}, u32[]{:S(2)}) collective-permute-start(f32[2,4,10,1,128]{4,3,2,1,0:T(1,128)S(1)} %get-tuple-element.40), channel_id=1, source_target_pairs={{0,1},{1,2},{2,3},{4,5},{5,6},{6,7},{8,9},{9,10},{10,11},{12,13},{... | collective-permute-start | bytes 122888 | tf_op jit(solution)/shard_map/ppermute | solution.py:17
  363.4 13.3 %collective-permute-start.33 = (f32[2,4,1,16,128]{4,3,2,1,0:T(8,128)S(1)}, f32[2,4,1,16,128]{4,3,2,1,0:T(8,128)S(1)}, u32[]{:S(2)}, u32[]{:S(2)}) collective-permute-start(f32[2,4,1,16,128]{4,3,2,1,0:T(8,128)S(1)} %get-tuple-element.67), channel_id=1, source_target_pairs={{0,4},{4,8},{8,12},{12,16},{16,20},{20,24},{24,28},{1,5},{5,9},{9,... | collective-permute-start | bytes 196616 | tf_op jit(solution)/shard_map/ppermute | solution.py:17
  366.6 10.1 %collective-permute-start.32 = (f32[2,4,1,16,128]{4,3,2,1,0:T(8,128)S(1)}, f32[2,4,1,16,128]{4,3,2,1,0:T(8,128)S(1)}, u32[]{:S(2)}, u32[]{:S(2)}) collective-permute-start(f32[2,4,1,16,128]{4,3,2,1,0:T(8,128)S(1)} %get-tuple-element.68), channel_id=1, source_target_pairs={{4,0},{8,4},{12,8},{16,12},{20,16},{24,20},{28,24},{5,1},{9,5},{13... | collective-permute-start | bytes 196616 | tf_op jit(solution)/shard_map/ppermute | solution.py:18
  368.5 31.4 %collective-permute-start.53 = (f32[1,16,128]{1,2,0:T(8,128)}, f32[1,16,128]{1,2,0:T(8,128)}, u32[]{:S(2)}, u32[]{:S(2)}) collective-permute-start(f32[1,16,128]{1,2,0:T(8,128)} %bitcast.29), channel_id=1, source_target_pairs={{0,4},{4,8},{8,12},{12,16},{16,20},{20,24},{24,28},{1,5},{5,9},{9,... | collective-permute-start | bytes 24584 | tf_op jit(solution)/shard_map/ppermute | solution.py:17
  374.6 44.7 %collective-permute-start.56 = (f32[1,16,128]{1,2,0:T(8,128)}, f32[1,16,128]{1,2,0:T(8,128)}, u32[]{:S(2)}, u32[]{:S(2)}) collective-permute-start(f32[1,16,128]{1,2,0:T(8,128)} %bitcast.38), channel_id=1, source_target_pairs={{4,0},{8,4},{12,8},{16,12},{20,16},{24,20},{28,24},{5,1},{9,5},{13... | collective-permute-start | bytes 24584 | tf_op jit(solution)/shard_map/ppermute | solution.py:18
  376.9 5.9 %collective-permute-start.34 = (f32[2,4,10,1,128]{4,3,2,1,0:T(1,128)S(1)}, f32[2,4,10,1,128]{4,3,2,1,0:T(1,128)S(1)}, u32[]{:S(2)}, u32[]{:S(2)}) collective-permute-start(f32[2,4,10,1,128]{4,3,2,1,0:T(1,128)S(1)} %get-tuple-element.37), channel_id=1, source_target_pairs={{1,0},{2,1},{3,2},{5,4},{6,5},{7,6},{9,8},{10,9},{11,10},{13,12},{... | collective-permute-start | bytes 122888 | tf_op jit(solution)/shard_map/ppermute | solution.py:18
  378.8 5.9 %collective-permute-start.35 = (f32[2,4,10,1,128]{4,3,2,1,0:T(1,128)S(1)}, f32[2,4,10,1,128]{4,3,2,1,0:T(1,128)S(1)}, u32[]{:S(2)}, u32[]{:S(2)}) collective-permute-start(f32[2,4,10,1,128]{4,3,2,1,0:T(1,128)S(1)} %get-tuple-element.38), channel_id=1, source_target_pairs={{0,1},{1,2},{2,3},{4,5},{5,6},{6,7},{8,9},{9,10},{10,11},{12,13},{... | collective-permute-start | bytes 122888 | tf_op jit(solution)/shard_map/ppermute | solution.py:17
  386.6 16.7 %collective-permute-start.37 = (f32[2,4,1,16,128]{4,3,2,1,0:T(8,128)}, f32[2,4,1,16,128]{4,3,2,1,0:T(8,128)S(1)}, u32[]{:S(2)}, u32[]{:S(2)}) collective-permute-start(f32[2,4,1,16,128]{4,3,2,1,0:T(8,128)} %get-tuple-element.65), channel_id=1, source_target_pairs={{0,4},{4,8},{8,12},{12,16},{16,20},{20,24},{24,28},{1,5},{5,9},{9,... | collective-permute-start | bytes 196616 | tf_op jit(solution)/shard_map/ppermute | solution.py:17
  391.1 12.2 %collective-permute-start.36 = (f32[2,4,1,16,128]{4,3,2,1,0:T(8,128)S(1)}, f32[2,4,1,16,128]{4,3,2,1,0:T(8,128)S(1)}, u32[]{:S(2)}, u32[]{:S(2)}) collective-permute-start(f32[2,4,1,16,128]{4,3,2,1,0:T(8,128)S(1)} %get-tuple-element.66), channel_id=1, source_target_pairs={{4,0},{8,4},{12,8},{16,12},{20,16},{24,20},{28,24},{5,1},{9,5},{13... | collective-permute-start | bytes 196616 | tf_op jit(solution)/shard_map/ppermute | solution.py:18
  393.1 31.6 %collective-permute-start.57 = (f32[1,16,128]{1,2,0:T(8,128)}, f32[1,16,128]{1,2,0:T(8,128)}, u32[]{:S(2)}, u32[]{:S(2)}) collective-permute-start(f32[1,16,128]{1,2,0:T(8,128)} %bitcast.39), channel_id=1, source_target_pairs={{0,4},{4,8},{8,12},{12,16},{16,20},{20,24},{24,28},{1,5},{5,9},{9,... | collective-permute-start | bytes 24584 | tf_op jit(solution)/shard_map/ppermute | solution.py:17
  399.9 62.7 %collective-permute-start.50 = (f32[10,1,128]{2,1,0:T(1,128)}, f32[10,1,128]{2,1,0:T(1,128)}, u32[]{:S(2)}, u32[]{:S(2)}) collective-permute-start(f32[10,1,128]{2,1,0:T(1,128)} %get-tuple-element.97), channel_id=1, source_target_pairs={{1,0},{2,1},{3,2},{5,4},{6,5},{7,6},{9,8},{10,9},{11,10},{13,12},{... | collective-permute-start | bytes 15368 | tf_op jit(solution)/shard_map/ppermute | solution.py:18
  403.4 6.0 %collective-permute-start.38 = (f32[2,4,10,1,128]{4,3,2,1,0:T(1,128)S(1)}, f32[2,4,10,1,128]{4,3,2,1,0:T(1,128)S(1)}, u32[]{:S(2)}, u32[]{:S(2)}) collective-permute-start(f32[2,4,10,1,128]{4,3,2,1,0:T(1,128)S(1)} %get-tuple-element.35), channel_id=1, source_target_pairs={{1,0},{2,1},{3,2},{5,4},{6,5},{7,6},{9,8},{10,9},{11,10},{13,12},{... | collective-permute-start | bytes 122888 | tf_op jit(solution)/shard_map/ppermute | solution.py:18
  405.3 5.9 %collective-permute-start.39 = (f32[2,4,10,1,128]{4,3,2,1,0:T(1,128)S(1)}, f32[2,4,10,1,128]{4,3,2,1,0:T(1,128)S(1)}, u32[]{:S(2)}, u32[]{:S(2)}) collective-permute-start(f32[2,4,10,1,128]{4,3,2,1,0:T(1,128)S(1)} %get-tuple-element.36), channel_id=1, source_target_pairs={{0,1},{1,2},{2,3},{4,5},{5,6},{6,7},{8,9},{9,10},{10,11},{12,13},{... | collective-permute-start | bytes 122888 | tf_op jit(solution)/shard_map/ppermute | solution.py:17
  413.1 15.6 %collective-permute-start.41 = (f32[2,4,1,16,128]{4,3,2,1,0:T(8,128)}, f32[2,4,1,16,128]{4,3,2,1,0:T(8,128)S(1)}, u32[]{:S(2)}, u32[]{:S(2)}) collective-permute-start(f32[2,4,1,16,128]{4,3,2,1,0:T(8,128)} %get-tuple-element.63), channel_id=1, source_target_pairs={{0,4},{4,8},{8,12},{12,16},{16,20},{20,24},{24,28},{1,5},{5,9},{9,... | collective-permute-start | bytes 196616 | tf_op jit(solution)/shard_map/ppermute | solution.py:17
  417.3 11.4 %collective-permute-start.40 = (f32[2,4,1,16,128]{4,3,2,1,0:T(8,128)}, f32[2,4,1,16,128]{4,3,2,1,0:T(8,128)S(1)}, u32[]{:S(2)}, u32[]{:S(2)}) collective-permute-start(f32[2,4,1,16,128]{4,3,2,1,0:T(8,128)} %get-tuple-element.64), channel_id=1, source_target_pairs={{4,0},{8,4},{12,8},{16,12},{20,16},{24,20},{28,24},{5,1},{9,5},{13... | collective-permute-start | bytes 196616 | tf_op jit(solution)/shard_map/ppermute | solution.py:18
  419.2 47.5 %collective-permute-start.51 = (f32[10,1,128]{2,1,0:T(1,128)}, f32[10,1,128]{2,1,0:T(1,128)}, u32[]{:S(2)}, u32[]{:S(2)}) collective-permute-start(f32[10,1,128]{2,1,0:T(1,128)} %get-tuple-element.98), channel_id=1, source_target_pairs={{0,1},{1,2},{2,3},{4,5},{5,6},{6,7},{8,9},{9,10},{10,11},{12,13},{... | collective-permute-start | bytes 15368 | tf_op jit(solution)/shard_map/ppermute | solution.py:17
  424.7 42.0 %collective-permute-start.54 = (f32[10,1,128]{2,1,0:T(1,128)}, f32[10,1,128]{2,1,0:T(1,128)}, u32[]{:S(2)}, u32[]{:S(2)}) collective-permute-start(f32[10,1,128]{2,1,0:T(1,128)} %get-tuple-element.99), channel_id=1, source_target_pairs={{1,0},{2,1},{3,2},{5,4},{6,5},{7,6},{9,8},{10,9},{11,10},{13,12},{... | collective-permute-start | bytes 15368 | tf_op jit(solution)/shard_map/ppermute | solution.py:18
  428.7 6.0 %collective-permute-start.42 = (f32[2,4,10,1,128]{4,3,2,1,0:T(1,128)S(1)}, f32[2,4,10,1,128]{4,3,2,1,0:T(1,128)S(1)}, u32[]{:S(2)}, u32[]{:S(2)}) collective-permute-start(f32[2,4,10,1,128]{4,3,2,1,0:T(1,128)S(1)} %get-tuple-element.33), channel_id=1, source_target_pairs={{1,0},{2,1},{3,2},{5,4},{6,5},{7,6},{9,8},{10,9},{11,10},{13,12},{... | collective-permute-start | bytes 122888 | tf_op jit(solution)/shard_map/ppermute | solution.py:18
  430.7 5.9 %collective-permute-start.43 = (f32[2,4,10,1,128]{4,3,2,1,0:T(1,128)S(1)}, f32[2,4,10,1,128]{4,3,2,1,0:T(1,128)S(1)}, u32[]{:S(2)}, u32[]{:S(2)}) collective-permute-start(f32[2,4,10,1,128]{4,3,2,1,0:T(1,128)S(1)} %get-tuple-element.34), channel_id=1, source_target_pairs={{0,1},{1,2},{2,3},{4,5},{5,6},{6,7},{8,9},{9,10},{10,11},{12,13},{... | collective-permute-start | bytes 122888 | tf_op jit(solution)/shard_map/ppermute | solution.py:17
  437.3 6.6 %collective-permute-start.45 = (f32[2,4,1,16,128]{4,3,2,1,0:T(8,128)S(1)}, f32[2,4,1,16,128]{4,3,2,1,0:T(8,128)S(1)}, u32[]{:S(2)}, u32[]{:S(2)}) collective-permute-start(f32[2,4,1,16,128]{4,3,2,1,0:T(8,128)S(1)} %get-tuple-element.61), channel_id=1, source_target_pairs={{0,4},{4,8},{8,12},{12,16},{16,20},{20,24},{24,28},{1,5},{5,9},{9,... | collective-permute-start | bytes 196616 | tf_op jit(solution)/shard_map/ppermute | solution.py:17
  442.0 6.2 %collective-permute-start.44 = (f32[2,4,1,16,128]{4,3,2,1,0:T(8,128)S(1)}, f32[2,4,1,16,128]{4,3,2,1,0:T(8,128)S(1)}, u32[]{:S(2)}, u32[]{:S(2)}) collective-permute-start(f32[2,4,1,16,128]{4,3,2,1,0:T(8,128)S(1)} %get-tuple-element.62), channel_id=1, source_target_pairs={{4,0},{8,4},{12,8},{16,12},{20,16},{24,20},{28,24},{5,1},{9,5},{13... | collective-permute-start | bytes 196616 | tf_op jit(solution)/shard_map/ppermute | solution.py:18
  448.3 6.1 %collective-permute-start.46 = (f32[2,4,10,1,128]{4,3,2,1,0:T(1,128)S(1)}, f32[2,4,10,1,128]{4,3,2,1,0:T(1,128)S(1)}, u32[]{:S(2)}, u32[]{:S(2)}) collective-permute-start(f32[2,4,10,1,128]{4,3,2,1,0:T(1,128)S(1)} %get-tuple-element.31), channel_id=1, source_target_pairs={{1,0},{2,1},{3,2},{5,4},{6,5},{7,6},{9,8},{10,9},{11,10},{13,12},{... | collective-permute-start | bytes 122888 | tf_op jit(solution)/shard_map/ppermute | solution.py:18
  450.3 8.1 %collective-permute-start.47 = (f32[2,4,10,1,128]{4,3,2,1,0:T(1,128)S(1)}, f32[2,4,10,1,128]{4,3,2,1,0:T(1,128)S(1)}, u32[]{:S(2)}, u32[]{:S(2)}) collective-permute-start(f32[2,4,10,1,128]{4,3,2,1,0:T(1,128)S(1)} %get-tuple-element.32), channel_id=1, source_target_pairs={{0,1},{1,2},{2,3},{4,5},{5,6},{6,7},{8,9},{9,10},{10,11},{12,13},{... | collective-permute-start | bytes 122888 | tf_op jit(solution)/shard_map/ppermute | solution.py:17
  454.3 12.4 %collective-permute-start.55 = (f32[10,1,128]{2,1,0:T(1,128)S(1)}, f32[10,1,128]{2,1,0:T(1,128)S(1)}, u32[]{:S(2)}, u32[]{:S(2)}) collective-permute-start(f32[10,1,128]{2,1,0:T(1,128)S(1)} %copy-done.107), channel_id=1, source_target_pairs={{0,1},{1,2},{2,3},{4,5},{5,6},{6,7},{8,9},{9,10},{10,11},{12,13},{... | collective-permute-start | bytes 15368 | tf_op jit(solution)/shard_map/ppermute | solution.py:17
  458.5 8.2 %collective-permute-start.58 = (f32[10,1,128]{2,1,0:T(1,128)S(1)}, f32[10,1,128]{2,1,0:T(1,128)S(1)}, u32[]{:S(2)}, u32[]{:S(2)}) collective-permute-start(f32[10,1,128]{2,1,0:T(1,128)S(1)} %get-tuple-element.101), channel_id=1, source_target_pairs={{1,0},{2,1},{3,2},{5,4},{6,5},{7,6},{9,8},{10,9},{11,10},{13,12},{... | collective-permute-start | bytes 15368 | tf_op jit(solution)/shard_map/ppermute | solution.py:18
  462.6 5.5 %collective-permute-start.59 = (f32[10,1,128]{2,1,0:T(1,128)S(1)}, f32[10,1,128]{2,1,0:T(1,128)S(1)}, u32[]{:S(2)}, u32[]{:S(2)}) collective-permute-start(f32[10,1,128]{2,1,0:T(1,128)S(1)} %get-tuple-element.102), channel_id=1, source_target_pairs={{0,1},{1,2},{2,3},{4,5},{5,6},{6,7},{8,9},{9,10},{10,11},{12,13},{... | collective-permute-start | bytes 15368 | tf_op jit(solution)/shard_map/ppermute | solution.py:17
  (108 other events, 981.6 us)
Sparse Core Ops, SparseCore 0:
  470.3 34.7 reduce-scatter.3
where the time goes:
time: 516 us; the launch traced here: 513 us
  blocking collectives  187 us (36%)
  starting transfers between devices  177 us (34%)
  waiting for transfers between devices  80.4 us (16%)
  local copies, waits for them, and re-layouts  31.7 us (6%)
  other arithmetic  21.6 us (4%)
  between operations  16.7 us (3%)
    ppermute x30, starting transfers between devices, padded_2(): before = lax.ppermute(last, axis, up)  127 us
    ppermute x30, starting transfers between devices, padded_2(): after = lax.ppermute(initial, axis, down)  49.5 us
    all_gather x3, blocking collectives, local(): lax.all_gather(saved_pore_load[backward_counter], 'obs', axis=2, tiled=True)  48.9 us
    all_gather x3, blocking collectives, local(): lax.all_gather(saved_heat_field[backward_counter], 'obs', axis=2, tiled=T...  46.9 us
    all_gather x3, blocking collectives, local(): lax.all_gather(saved_dilatation[backward_counter], 'obs', axis=2, tiled=T...  45.5 us
    all_gather x3, blocking collectives, local(): lax.all_gather(saved_conductivity[backward_counter], 'obs', axis=2, tiled...  45.3 us
    unnamed x2, waiting for transfers between devices  33.1 us
    ppermute x30, waiting for transfers between devices, padded_2(): after = lax.ppermute(initial, axis, down)  24.2 us
  transfers between devices with their start and end apart: 61, of which 22 were waited for; matrix products, arithmetic and copies ran while one was open for 8% of the time, Pallas kernels for 0%

commit v1 on v0

--- a/solution.py
+++ b/solution.py
@@ -69,7 +69,15 @@
         pressure_now, present_heat_field, strain_now, perm_now = (
             lax.all_gather(saved_pore_load[backward_counter], "obs", axis=2, tiled=True),
             lax.all_gather(saved_heat_field[backward_counter], "obs", axis=2, tiled=True),
-            lax.all_gather(saved_dilatation[backward_counter], "obs", axis=2, tiled=True),
+            jnp.concatenate(
+                lax.all_to_all(
+                    jnp.stack([saved_dilatation[backward_counter]] * lax.axis_size("obs")),
+                    "obs",
+                    0,
+                    0,
+                ),
+                axis=2,
+            ),
             lax.all_gather(saved_conductivity[backward_counter], "obs", axis=2, tiled=True),
         )
         store_p = jnp.exp(strain_now)

time: 516 us -> 487 us (0.944)
  blocking collectives: 187 us -> 145 us
  starting transfers between devices: 177 us -> 207 us
  waiting for transfers between devices: 80.4 us -> 68.9 us
  local copies, waits for them, and re-layouts: 31.7 us -> 25.8 us
    all_gather x3 -> x0, blocking collectives: 45.5 us -> none  [local(): lax.all_gather(saved_dilatation[backward_counter], 'obs', axis=2, tiled=T...]
    ppermute x30, waiting for transfers between devices: 24.2 us -> 1.07 us  [padded_2(): after = lax.ppermute(initial, axis, down)]
    all_to_all x0 -> x3, starting transfers between devices: none -> 16.4 us  [local(): lax.all_to_all(jnp.stack([saved_dilatation[backward_counter]] * lax.axis_...]
    ppermute x30, starting transfers between devices: 127 us -> 140 us  [padded_2(): before = lax.ppermute(last, axis, up)]
    unnamed x2, waiting for transfers between devices: 33.1 us -> 42 us
    ppermute x6 -> x0, local copies, waits for them, and re-layouts: 7.8 us -> none  [the longest x3 3.9 us: padded_2(): before = lax.ppermute(last, axis, up)]
    all_gather x3, blocking collectives: 45.3 us -> 51.5 us  [local(): lax.all_gather(saved_conductivity[backward_counter], 'obs', axis=2, tiled...]
    unnamed x240 -> x181, local copies, waits for them, and re-layouts: 12.5 us -> 12.8 us
  transfers between devices with their start and end apart: 61 -> 64, of which waited for: 22 -> 21; matrix products, arithmetic and copies ran while one was open for 8% -> 8% of each run, Pallas kernels for 0% -> 0%
where the time goes in v1:
time: 487 us; the launch traced here: 484 us
  starting transfers between devices  207 us (43%)
  blocking collectives  145 us (30%)
  waiting for transfers between devices  68.9 us (14%)
  local copies, waits for them, and re-layouts  25.8 us (5%)
  other arithmetic  21.3 us (4%)
  between operations  16.5 us (3%)
    ppermute x30, starting transfers between devices, padded_2(): before = lax.ppermute(last, axis, up)  140 us
    all_gather x3, blocking collectives, local(): lax.all_gather(saved_conductivity[backward_counter], 'obs', axis=2, tiled...  51.5 us
    ppermute x30, starting transfers between devices, padded_2(): after = lax.ppermute(initial, axis, down)  49.9 us
    all_gather x3, blocking collectives, local(): lax.all_gather(saved_pore_load[backward_counter], 'obs', axis=2, tiled=True)  48 us
    all_gather x3, blocking collectives, local(): lax.all_gather(saved_heat_field[backward_counter], 'obs', axis=2, tiled=T...  45.4 us
    unnamed x2, waiting for transfers between devices  42 us
    ppermute x30, waiting for transfers between devices, padded_2(): before = lax.ppermute(last, axis, up)  25.7 us
    all_to_all x3, starting transfers between devices, local(): lax.all_to_all(jnp.stack([saved_dilatation[backward_counter]] * lax.axis_...  16.4 us
  transfers between devices with their start and end apart: 64, of which 21 were waited for; matrix products, arithmetic and copies ran while one was open for 8% of the time, Pallas kernels for 0%

profile of v1, /device:TPU:2, one launch (start us, length us, event | category | flops | bytes accessed | tf_op | source)
XLA Modules:
  0.0 484.0 jit_solution(13847571004765425254)
XLA Ops:
  8.1 3.8 collective-permute-start.1
  14.2 7.6 %all-to-all-start.2 = ((f32[8,1,2048]{2,1,0:T(1,128)}), f32[8,1,2048]{2,1,0:T(1,128)S(1)}, u32[]{:S(2)}, u32[]{:S(2)}) async-start(f32[8,1,2048]{2,1,0:T(1,128)} %reshape.147), calls=%async_computation.2 | async-start | bytes 131072 | tf_op jit(solution)/shard_map/all_to_all | solution.py:73
  21.9 17.6 %all-gather.1 = f32[1,8,16,128]{2,1,0,3:T(8,128)S(1)} all-gather(f32[1,8,16,16]{2,1,0,3:T(8,128)S(1)} %copy.134), channel_id=3, replica_groups=mesh['obs'=8,'gx'=8,'gy'=4] {'obs'}, dimensions={3}, use_global_device_ids=true | all-gather | bytes 73728 | tf_op jit(solution)/shard_map/all_gather | solution.py:70
  41.6 5.6 %collective-permute-start.49 = (f32[1,16,128]{2,1,0:T(8,128)}, f32[1,16,128]{2,1,0:T(8,128)}, u32[]{:S(2)}, u32[]{:S(2)}) collective-permute-start(f32[1,16,128]{2,1,0:T(8,128)} %get-tuple-element.97), channel_id=1, source_target_pairs={{0,4},{4,8},{8,12},{12,16},{16,20},{20,24},{24,28},{1,5},{5,9},{9,... | collective-permute-start | bytes 24584 | tf_op jit(solution)/shard_map/ppermute | solution.py:17
  47.3 15.2 %all-gather.4 = f32[1,8,16,128]{2,1,0,3:T(8,128)S(1)} all-gather(f32[1,8,16,16]{2,1,0,3:T(8,128)S(1)} %copy.137), channel_id=6, replica_groups=mesh['obs'=8,'gx'=8,'gy'=4] {'obs'}, dimensions={3}, use_global_device_ids=true | all-gather | bytes 73728 | tf_op jit(solution)/shard_map/all_gather | solution.py:70
  64.8 15.1 %all-gather.2 = f32[1,8,16,128]{2,1,0,3:T(8,128)S(1)} all-gather(f32[1,8,16,16]{2,1,0,3:T(8,128)S(1)} %copy.135), channel_id=4, replica_groups=mesh['obs'=8,'gx'=8,'gy'=4] {'obs'}, dimensions={3}, use_global_device_ids=true | all-gather | bytes 73728 | tf_op jit(solution)/shard_map/all_gather | solution.py:71
  81.0 15.2 %all-gather.5 = f32[1,8,16,128]{2,1,0,3:T(8,128)S(1)} all-gather(f32[1,8,16,16]{2,1,0,3:T(8,128)S(1)} %copy.138), channel_id=7, replica_groups=mesh['obs'=8,'gx'=8,'gy'=4] {'obs'}, dimensions={3}, use_global_device_ids=true | all-gather | bytes 73728 | tf_op jit(solution)/shard_map/all_gather | solution.py:71
  100.5 2.4 collective-permute-start.2
  103.0 3.4 collective-permute-start.3
  106.4 15.2 %all-gather = f32[1,8,16,128]{2,1,0,3:T(8,128)S(1)} all-gather(f32[1,8,16,16]{2,1,0,3:T(8,128)S(1)} %copy.133), channel_id=2, replica_groups=mesh['obs'=8,'gx'=8,'gy'=4] {'obs'}, dimensions={3}, use_global_device_ids=true | all-gather | bytes 73728 | tf_op jit(solution)/shard_map/all_gather | solution.py:81
  122.8 15.0 %all-gather.8 = f32[1,8,16,128]{2,1,0,3:T(8,128)S(1)} all-gather(f32[1,8,16,16]{2,1,0,3:T(8,128)S(1)} %copy.141), channel_id=10, replica_groups=mesh['obs'=8,'gx'=8,'gy'=4] {'obs'}, dimensions={3}, use_global_device_ids=true | all-gather | bytes 73728 | tf_op jit(solution)/shard_map/all_gather | solution.py:71
  138.4 4.5 all-to-all-start.1
  146.5 6.0 %collective-permute-start.5 = (f32[2,4,1,16,128]{4,3,2,1,0:T(8,128)S(1)}, f32[2,4,1,16,128]{4,3,2,1,0:T(8,128)S(1)}, u32[]{:S(2)}, u32[]{:S(2)}) collective-permute-start(f32[2,4,1,16,128]{4,3,2,1,0:T(8,128)S(1)} %get-tuple-element.75), channel_id=1, source_target_pairs={{0,4},{4,8},{8,12},{12,16},{16,20},{20,24},{24,28},{1,5},{5,9},{9,... | collective-permute-start | bytes 196616 | tf_op jit(solution)/shard_map/ppermute | solution.py:17
  154.6 2.4 collective-permute-start.6
  157.0 3.4 collective-permute-start.7
  160.5 2.4 collective-permute-done.7
  164.8 5.4 %collective-permute-start.9 = (f32[2,4,1,16,128]{4,3,2,1,0:T(8,128)S(1)}, f32[2,4,1,16,128]{4,3,2,1,0:T(8,128)S(1)}, u32[]{:S(2)}, u32[]{:S(2)}) collective-permute-start(f32[2,4,1,16,128]{4,3,2,1,0:T(8,128)S(1)} %get-tuple-element.73), channel_id=1, source_target_pairs={{0,4},{4,8},{8,12},{12,16},{16,20},{20,24},{24,28},{1,5},{5,9},{9,... | collective-permute-start | bytes 196616 | tf_op jit(solution)/shard_map/ppermute | solution.py:17
  170.9 17.6 %all-gather.3 = f32[1,8,16,128]{2,1,0,3:T(8,128)S(1)} all-gather(f32[1,8,16,16]{2,1,0,3:T(8,128)S(1)} %copy.136), channel_id=5, replica_groups=mesh['obs'=8,'gx'=8,'gy'=4] {'obs'}, dimensions={3}, use_global_device_ids=true | all-gather | bytes 73728 | tf_op jit(solution)/shard_map/all_gather | solution.py:81
  189.8 15.2 %all-gather.7 = f32[1,8,16,128]{2,1,0,3:T(8,128)S(1)} all-gather(f32[1,8,16,16]{2,1,0,3:T(8,128)S(1)} %copy.140), channel_id=9, replica_groups=mesh['obs'=8,'gx'=8,'gy'=4] {'obs'}, dimensions={3}, use_global_device_ids=true | all-gather | bytes 73728 | tf_op jit(solution)/shard_map/all_gather | solution.py:70
  205.8 4.4 all-to-all-start
  212.0 1.9 collective-permute-start.10
  213.9 4.1 collective-permute-start.11
  221.9 5.8 %collective-permute-start.13 = (f32[2,4,1,16,128]{4,3,2,1,0:T(8,128)S(1)}, f32[2,4,1,16,128]{4,3,2,1,0:T(8,128)S(1)}, u32[]{:S(2)}, u32[]{:S(2)}) collective-permute-start(f32[2,4,1,16,128]{4,3,2,1,0:T(8,128)S(1)} %get-tuple-element.71), channel_id=1, source_target_pairs={{0,4},{4,8},{8,12},{12,16},{16,20},{20,24},{24,28},{1,5},{5,9},{9,... | collective-permute-start | bytes 196616 | tf_op jit(solution)/shard_map/ppermute | solution.py:17
  229.7 1.9 collective-permute-start.14
  231.6 3.9 collective-permute-start.15
  235.6 1.9 collective-permute-done.15
  239.5 5.4 %collective-permute-start.17 = (f32[2,4,1,16,128]{4,3,2,1,0:T(8,128)S(1)}, f32[2,4,1,16,128]{4,3,2,1,0:T(8,128)S(1)}, u32[]{:S(2)}, u32[]{:S(2)}) collective-permute-start(f32[2,4,1,16,128]{4,3,2,1,0:T(8,128)S(1)} %get-tuple-element.69), channel_id=1, source_target_pairs={{0,4},{4,8},{8,12},{12,16},{16,20},{20,24},{24,28},{1,5},{5,9},{9,... | collective-permute-start | bytes 196616 | tf_op jit(solution)/shard_map/ppermute | solution.py:17
  246.9 1.9 collective-permute-start.18
  248.8 3.9 collective-permute-start.19
  252.9 1.9 collective-permute-done.19
  257.3 5.8 %collective-permute-start.21 = (f32[2,4,1,16,128]{4,3,2,1,0:T(8,128)S(1)}, f32[2,4,1,16,128]{4,3,2,1,0:T(8,128)S(1)}, u32[]{:S(2)}, u32[]{:S(2)}) collective-permute-start(f32[2,4,1,16,128]{4,3,2,1,0:T(8,128)S(1)} %get-tuple-element.67), channel_id=1, source_target_pairs={{0,4},{4,8},{8,12},{12,16},{16,20},{20,24},{24,28},{1,5},{5,9},{9,... | collective-permute-start | bytes 196616 | tf_op jit(solution)/shard_map/ppermute | solution.py:17
  265.1 1.9 collective-permute-start.22
  267.0 3.9 collective-permute-start.23
  271.0 1.9 collective-permute-done.23
  276.0 5.8 %collective-permute-start.25 = (f32[2,4,1,16,128]{4,3,2,1,0:T(8,128)}, f32[2,4,1,16,128]{4,3,2,1,0:T(8,128)S(1)}, u32[]{:S(2)}, u32[]{:S(2)}) collective-permute-start(f32[2,4,1,16,128]{4,3,2,1,0:T(8,128)} %get-tuple-element.65), channel_id=1, source_target_pairs={{0,4},{4,8},{8,12},{12,16},{16,20},{20,24},{24,28},{1,5},{5,9},{9,... | collective-permute-start | bytes 196616 | tf_op jit(solution)/shard_map/ppermute | solution.py:17
  282.5 18.6 %all-gather.6 = f32[1,8,16,128]{2,1,0,3:T(8,128)} all-gather(f32[1,8,16,16]{2,1,0,3:T(8,128)S(1)} %copy.139), channel_id=8, replica_groups=mesh['obs'=8,'gx'=8,'gy'=4] {'obs'}, dimensions={3}, use_global_device_ids=true | all-gather | bytes 73728 | tf_op jit(solution)/shard_map/all_gather | solution.py:81
  301.2 1.9 copy.120
  306.2 1.9 collective-permute-start.26
  308.2 3.9 collective-permute-start.27
  316.7 5.6 %collective-permute-start.29 = (f32[2,4,1,16,128]{4,3,2,1,0:T(8,128)S(1)}, f32[2,4,1,16,128]{4,3,2,1,0:T(8,128)S(1)}, u32[]{:S(2)}, u32[]{:S(2)}) collective-permute-start(f32[2,4,1,16,128]{4,3,2,1,0:T(8,128)S(1)} %get-tuple-element.63), channel_id=1, source_target_pairs={{0,4},{4,8},{8,12},{12,16},{16,20},{20,24},{24,28},{1,5},{5,9},{9,... | collective-permute-start | bytes 196616 | tf_op jit(solution)/shard_map/ppermute | solution.py:17
  325.5 1.9 collective-permute-start.30
  327.4 3.9 collective-permute-start.31
  331.4 1.9 collective-permute-done.31
  335.4 5.4 %collective-permute-start.33 = (f32[2,4,1,16,128]{4,3,2,1,0:T(8,128)S(1)}, f32[2,4,1,16,128]{4,3,2,1,0:T(8,128)S(1)}, u32[]{:S(2)}, u32[]{:S(2)}) collective-permute-start(f32[2,4,1,16,128]{4,3,2,1,0:T(8,128)S(1)} %get-tuple-element.61), channel_id=1, source_target_pairs={{0,4},{4,8},{8,12},{12,16},{16,20},{20,24},{24,28},{1,5},{5,9},{9,... | collective-permute-start | bytes 196616 | tf_op jit(solution)/shard_map/ppermute | solution.py:17
  342.8 1.9 collective-permute-start.34
  344.8 4.1 collective-permute-start.35
  348.9 4.8 collective-permute-start.53
  357.8 6.4 %collective-permute-start.37 = (f32[2,4,1,16,128]{4,3,2,1,0:T(8,128)S(1)}, f32[2,4,1,16,128]{4,3,2,1,0:T(8,128)S(1)}, u32[]{:S(2)}, u32[]{:S(2)}) collective-permute-start(f32[2,4,1,16,128]{4,3,2,1,0:T(8,128)S(1)} %get-tuple-element.59), channel_id=1, source_target_pairs={{0,4},{4,8},{8,12},{12,16},{16,20},{20,24},{24,28},{1,5},{5,9},{9,... | collective-permute-start | bytes 196616 | tf_op jit(solution)/shard_map/ppermute | solution.py:17
  366.2 1.9 collective-permute-start.38
  368.1 3.9 collective-permute-start.39
  372.1 4.8 collective-permute-start.57
  377.0 1.9 collective-permute-start.50
  380.9 5.8 %collective-permute-start.41 = (f32[2,4,1,16,128]{4,3,2,1,0:T(8,128)S(1)}, f32[2,4,1,16,128]{4,3,2,1,0:T(8,128)S(1)}, u32[]{:S(2)}, u32[]{:S(2)}) collective-permute-start(f32[2,4,1,16,128]{4,3,2,1,0:T(8,128)S(1)} %get-tuple-element.57), channel_id=1, source_target_pairs={{0,4},{4,8},{8,12},{12,16},{16,20},{20,24},{24,28},{1,5},{5,9},{9,... | collective-permute-start | bytes 196616 | tf_op jit(solution)/shard_map/ppermute | solution.py:17
  388.6 1.9 collective-permute-start.42
  390.6 3.9 collective-permute-start.43
  394.5 3.9 collective-permute-start.51
  398.5 1.9 collective-permute-start.54
  402.4 5.5 %collective-permute-start.45 = (f32[2,4,1,16,128]{4,3,2,1,0:T(8,128)S(1)}, f32[2,4,1,16,128]{4,3,2,1,0:T(8,128)S(1)}, u32[]{:S(2)}, u32[]{:S(2)}) collective-permute-start(f32[2,4,1,16,128]{4,3,2,1,0:T(8,128)S(1)} %get-tuple-element.55), channel_id=1, source_target_pairs={{0,4},{4,8},{8,12},{12,16},{16,20},{20,24},{24,28},{1,5},{5,9},{9,... | collective-permute-start | bytes 196616 | tf_op jit(solution)/shard_map/ppermute | solution.py:17
  409.8 1.9 collective-permute-start.46
  411.7 4.1 collective-permute-start.47
  416.0 4.0 collective-permute-start.55
  420.1 2.1 collective-permute-start.58
  424.1 3.9 collective-permute-start.59
  433.6 42.0 %reduce-scatter.4.cloned.1.call-done = f32[16,128]{1,0:T(8,128)} async-done(((f32[128,128]{1,0:T(8,128)}), f32[16,128]{1,0:T(8,128)}) %reduce-scatter.4.cloned.1.call-update) | async-done | bytes 8208
  (372 shorter events, 82.0 us)
Async XLA Ops:
  8.1 92.2 %collective-permute-start.1 = (f32[2,4,1,16,128]{4,3,2,1,0:T(8,128)S(1)}, f32[2,4,1,16,128]{4,3,2,1,0:T(8,128)S(1)}, u32[]{:S(2)}, u32[]{:S(2)}) collective-permute-start(f32[2,4,1,16,128]{4,3,2,1,0:T(8,128)S(1)} %get-tuple-element.78), channel_id=1, source_target_pairs={{0,4},{4,8},{8,12},{12,16},{16,20},{20,24},{24,28},{1,5},{5,9},{9,... | collective-permute-start | bytes 196616 | tf_op jit(solution)/shard_map/ppermute | solution.py:17
  11.9 88.5 %collective-permute-start = (f32[2,4,1,16,128]{4,3,2,1,0:T(8,128)S(1)}, f32[2,4,1,16,128]{4,3,2,1,0:T(8,128)S(1)}, u32[]{:S(2)}, u32[]{:S(2)}) collective-permute-start(f32[2,4,1,16,128]{4,3,2,1,0:T(8,128)S(1)} %get-tuple-element.77), channel_id=1, source_target_pairs={{4,0},{8,4},{12,8},{16,12},{20,16},{24,20},{28,24},{5,1},{9,5},{13... | collective-permute-start | bytes 196616 | tf_op jit(solution)/shard_map/ppermute | solution.py:18
  14.2 124.2 %all-to-all-start.2 = ((f32[8,1,2048]{2,1,0:T(1,128)}), f32[8,1,2048]{2,1,0:T(1,128)S(1)}, u32[]{:S(2)}, u32[]{:S(2)}) async-start(f32[8,1,2048]{2,1,0:T(1,128)} %reshape.147), calls=%async_computation.2 | async-start | bytes 131072 | tf_op jit(solution)/shard_map/all_to_all | solution.py:73
  40.3 316.2 %collective-permute-start.48 = (f32[1,16,128]{2,1,0:T(8,128)}, f32[1,16,128]{2,1,0:T(8,128)}, u32[]{:S(2)}, u32[]{:S(2)}) collective-permute-start(f32[1,16,128]{2,1,0:T(8,128)} %get-tuple-element.98), channel_id=1, source_target_pairs={{4,0},{8,4},{12,8},{16,12},{20,16},{24,20},{28,24},{5,1},{9,5},{13... | collective-permute-start | bytes 24584 | tf_op jit(solution)/shard_map/ppermute | solution.py:18
  41.6 316.2 %collective-permute-start.49 = (f32[1,16,128]{2,1,0:T(8,128)}, f32[1,16,128]{2,1,0:T(8,128)}, u32[]{:S(2)}, u32[]{:S(2)}) collective-permute-start(f32[1,16,128]{2,1,0:T(8,128)} %get-tuple-element.97), channel_id=1, source_target_pairs={{0,4},{4,8},{8,12},{12,16},{16,20},{20,24},{24,28},{1,5},{5,9},{9,... | collective-permute-start | bytes 24584 | tf_op jit(solution)/shard_map/ppermute | solution.py:17
  63.4 316.2 %collective-permute-start.52 = (f32[1,16,128]{2,1,0:T(8,128)}, f32[1,16,128]{2,1,0:T(8,128)}, u32[]{:S(2)}, u32[]{:S(2)}) collective-permute-start(f32[1,16,128]{2,1,0:T(8,128)} %get-tuple-element.100), channel_id=1, source_target_pairs={{4,0},{8,4},{12,8},{16,12},{20,16},{24,20},{28,24},{5,1},{9,5},{13... | collective-permute-start | bytes 24584 | tf_op jit(solution)/shard_map/ppermute | solution.py:18
  100.5 37.5 %collective-permute-start.2 = (f32[2,4,10,1,128]{4,3,2,1,0:T(1,128)S(1)}, f32[2,4,10,1,128]{4,3,2,1,0:T(1,128)S(1)}, u32[]{:S(2)}, u32[]{:S(2)}) collective-permute-start(f32[2,4,10,1,128]{4,3,2,1,0:T(1,128)S(1)} %get-tuple-element.53), channel_id=1, source_target_pairs={{1,0},{2,1},{3,2},{5,4},{6,5},{7,6},{9,8},{10,9},{11,10},{13,12},{... | collective-permute-start | bytes 122888 | tf_op jit(solution)/shard_map/ppermute | solution.py:18
  103.0 35.1 %collective-permute-start.3 = (f32[2,4,10,1,128]{4,3,2,1,0:T(1,128)S(1)}, f32[2,4,10,1,128]{4,3,2,1,0:T(1,128)S(1)}, u32[]{:S(2)}, u32[]{:S(2)}) collective-permute-start(f32[2,4,10,1,128]{4,3,2,1,0:T(1,128)S(1)} %get-tuple-element.54), channel_id=1, source_target_pairs={{0,1},{1,2},{2,3},{4,5},{5,6},{6,7},{8,9},{9,10},{10,11},{12,13},{... | collective-permute-start | bytes 122888 | tf_op jit(solution)/shard_map/ppermute | solution.py:17
  138.4 67.4 %all-to-all-start.1 = ((f32[8,1,2048]{2,1,0:T(1,128)}), f32[8,1,2048]{2,1,0:T(1,128)S(1)}, u32[]{:S(2)}, u32[]{:S(2)}) async-start(f32[8,1,2048]{2,1,0:T(1,128)} %reshape.149), calls=%async_computation.1 | async-start | bytes 131072 | tf_op jit(solution)/shard_map/all_to_all | solution.py:73
  145.2 8.1 %collective-permute-start.4 = (f32[2,4,1,16,128]{4,3,2,1,0:T(8,128)S(1)}, f32[2,4,1,16,128]{4,3,2,1,0:T(8,128)S(1)}, u32[]{:S(2)}, u32[]{:S(2)}) collective-permute-start(f32[2,4,1,16,128]{4,3,2,1,0:T(8,128)S(1)} %get-tuple-element.76), channel_id=1, source_target_pairs={{4,0},{8,4},{12,8},{16,12},{20,16},{24,20},{28,24},{5,1},{9,5},{13... | collective-permute-start | bytes 196616 | tf_op jit(solution)/shard_map/ppermute | solution.py:18
  146.5 8.0 %collective-permute-start.5 = (f32[2,4,1,16,128]{4,3,2,1,0:T(8,128)S(1)}, f32[2,4,1,16,128]{4,3,2,1,0:T(8,128)S(1)}, u32[]{:S(2)}, u32[]{:S(2)}) collective-permute-start(f32[2,4,1,16,128]{4,3,2,1,0:T(8,128)S(1)} %get-tuple-element.75), channel_id=1, source_target_pairs={{0,4},{4,8},{8,12},{12,16},{16,20},{20,24},{24,28},{1,5},{5,9},{9,... | collective-permute-start | bytes 196616 | tf_op jit(solution)/shard_map/ppermute | solution.py:17
  154.6 5.9 %collective-permute-start.6 = (f32[2,4,10,1,128]{4,3,2,1,0:T(1,128)S(1)}, f32[2,4,10,1,128]{4,3,2,1,0:T(1,128)S(1)}, u32[]{:S(2)}, u32[]{:S(2)}) collective-permute-start(f32[2,4,10,1,128]{4,3,2,1,0:T(1,128)S(1)} %get-tuple-element.51), channel_id=1, source_target_pairs={{1,0},{2,1},{3,2},{5,4},{6,5},{7,6},{9,8},{10,9},{11,10},{13,12},{... | collective-permute-start | bytes 122888 | tf_op jit(solution)/shard_map/ppermute | solution.py:18
  157.0 5.9 %collective-permute-start.7 = (f32[2,4,10,1,128]{4,3,2,1,0:T(1,128)S(1)}, f32[2,4,10,1,128]{4,3,2,1,0:T(1,128)S(1)}, u32[]{:S(2)}, u32[]{:S(2)}) collective-permute-start(f32[2,4,10,1,128]{4,3,2,1,0:T(1,128)S(1)} %get-tuple-element.52), channel_id=1, source_target_pairs={{0,1},{1,2},{2,3},{4,5},{5,6},{6,7},{8,9},{9,10},{10,11},{12,13},{... | collective-permute-start | bytes 122888 | tf_op jit(solution)/shard_map/ppermute | solution.py:17
  163.5 48.4 %collective-permute-start.8 = (f32[2,4,1,16,128]{4,3,2,1,0:T(8,128)S(1)}, f32[2,4,1,16,128]{4,3,2,1,0:T(8,128)S(1)}, u32[]{:S(2)}, u32[]{:S(2)}) collective-permute-start(f32[2,4,1,16,128]{4,3,2,1,0:T(8,128)S(1)} %get-tuple-element.74), channel_id=1, source_target_pairs={{4,0},{8,4},{12,8},{16,12},{20,16},{24,20},{28,24},{5,1},{9,5},{13... | collective-permute-start | bytes 196616 | tf_op jit(solution)/shard_map/ppermute | solution.py:18
  164.8 47.1 %collective-permute-start.9 = (f32[2,4,1,16,128]{4,3,2,1,0:T(8,128)S(1)}, f32[2,4,1,16,128]{4,3,2,1,0:T(8,128)S(1)}, u32[]{:S(2)}, u32[]{:S(2)}) collective-permute-start(f32[2,4,1,16,128]{4,3,2,1,0:T(8,128)S(1)} %get-tuple-element.73), channel_id=1, source_target_pairs={{0,4},{4,8},{8,12},{12,16},{16,20},{20,24},{24,28},{1,5},{5,9},{9,... | collective-permute-start | bytes 196616 | tf_op jit(solution)/shard_map/ppermute | solution.py:17
  205.8 97.8 %all-to-all-start = ((f32[8,1,2048]{2,1,0:T(1,128)}), f32[8,1,2048]{2,1,0:T(1,128)}, u32[]{:S(2)}, u32[]{:S(2)}) async-start(f32[8,1,2048]{2,1,0:T(1,128)} %reshape.151), calls=%async_computation | async-start | bytes 131072 | tf_op jit(solution)/shard_map/all_to_all | solution.py:73
  210.2 265.5 %reduce-scatter.4.cloned.1.call-start = ((), (), s32[]{:S(2)}) async-start(), calls=%async_computation.4 | async-start | bytes 73728
  212.0 6.1 %collective-permute-start.10 = (f32[2,4,10,1,128]{4,3,2,1,0:T(1,128)S(1)}, f32[2,4,10,1,128]{4,3,2,1,0:T(1,128)S(1)}, u32[]{:S(2)}, u32[]{:S(2)}) collective-permute-start(f32[2,4,10,1,128]{4,3,2,1,0:T(1,128)S(1)} %get-tuple-element.49), channel_id=1, source_target_pairs={{1,0},{2,1},{3,2},{5,4},{6,5},{7,6},{9,8},{10,9},{11,10},{13,12},{... | collective-permute-start | bytes 122888 | tf_op jit(solution)/shard_map/ppermute | solution.py:18
  213.9 5.9 %collective-permute-start.11 = (f32[2,4,10,1,128]{4,3,2,1,0:T(1,128)S(1)}, f32[2,4,10,1,128]{4,3,2,1,0:T(1,128)S(1)}, u32[]{:S(2)}, u32[]{:S(2)}) collective-permute-start(f32[2,4,10,1,128]{4,3,2,1,0:T(1,128)S(1)} %get-tuple-element.50), channel_id=1, source_target_pairs={{0,1},{1,2},{2,3},{4,5},{5,6},{6,7},{8,9},{9,10},{10,11},{12,13},{... | collective-permute-start | bytes 122888 | tf_op jit(solution)/shard_map/ppermute | solution.py:17
  220.5 7.9 %collective-permute-start.12 = (f32[2,4,1,16,128]{4,3,2,1,0:T(8,128)S(1)}, f32[2,4,1,16,128]{4,3,2,1,0:T(8,128)S(1)}, u32[]{:S(2)}, u32[]{:S(2)}) collective-permute-start(f32[2,4,1,16,128]{4,3,2,1,0:T(8,128)S(1)} %get-tuple-element.72), channel_id=1, source_target_pairs={{4,0},{8,4},{12,8},{16,12},{20,16},{24,20},{28,24},{5,1},{9,5},{13... | collective-permute-start | bytes 196616 | tf_op jit(solution)/shard_map/ppermute | solution.py:18
  221.9 7.7 %collective-permute-start.13 = (f32[2,4,1,16,128]{4,3,2,1,0:T(8,128)S(1)}, f32[2,4,1,16,128]{4,3,2,1,0:T(8,128)S(1)}, u32[]{:S(2)}, u32[]{:S(2)}) collective-permute-start(f32[2,4,1,16,128]{4,3,2,1,0:T(8,128)S(1)} %get-tuple-element.71), channel_id=1, source_target_pairs={{0,4},{4,8},{8,12},{12,16},{16,20},{20,24},{24,28},{1,5},{5,9},{9,... | collective-permute-start | bytes 196616 | tf_op jit(solution)/shard_map/ppermute | solution.py:17
  229.7 5.9 %collective-permute-start.14 = (f32[2,4,10,1,128]{4,3,2,1,0:T(1,128)S(1)}, f32[2,4,10,1,128]{4,3,2,1,0:T(1,128)S(1)}, u32[]{:S(2)}, u32[]{:S(2)}) collective-permute-start(f32[2,4,10,1,128]{4,3,2,1,0:T(1,128)S(1)} %get-tuple-element.47), channel_id=1, source_target_pairs={{1,0},{2,1},{3,2},{5,4},{6,5},{7,6},{9,8},{10,9},{11,10},{13,12},{... | collective-permute-start | bytes 122888 | tf_op jit(solution)/shard_map/ppermute | solution.py:18
  231.6 5.9 %collective-permute-start.15 = (f32[2,4,10,1,128]{4,3,2,1,0:T(1,128)S(1)}, f32[2,4,10,1,128]{4,3,2,1,0:T(1,128)S(1)}, u32[]{:S(2)}, u32[]{:S(2)}) collective-permute-start(f32[2,4,10,1,128]{4,3,2,1,0:T(1,128)S(1)} %get-tuple-element.48), channel_id=1, source_target_pairs={{0,1},{1,2},{2,3},{4,5},{5,6},{6,7},{8,9},{9,10},{10,11},{12,13},{... | collective-permute-start | bytes 122888 | tf_op jit(solution)/shard_map/ppermute | solution.py:17
  238.2 7.1 %collective-permute-start.16 = (f32[2,4,1,16,128]{4,3,2,1,0:T(8,128)S(1)}, f32[2,4,1,16,128]{4,3,2,1,0:T(8,128)S(1)}, u32[]{:S(2)}, u32[]{:S(2)}) collective-permute-start(f32[2,4,1,16,128]{4,3,2,1,0:T(8,128)S(1)} %get-tuple-element.70), channel_id=1, source_target_pairs={{4,0},{8,4},{12,8},{16,12},{20,16},{24,20},{28,24},{5,1},{9,5},{13... | collective-permute-start | bytes 196616 | tf_op jit(solution)/shard_map/ppermute | solution.py:18
  239.5 7.3 %collective-permute-start.17 = (f32[2,4,1,16,128]{4,3,2,1,0:T(8,128)S(1)}, f32[2,4,1,16,128]{4,3,2,1,0:T(8,128)S(1)}, u32[]{:S(2)}, u32[]{:S(2)}) collective-permute-start(f32[2,4,1,16,128]{4,3,2,1,0:T(8,128)S(1)} %get-tuple-element.69), channel_id=1, source_target_pairs={{0,4},{4,8},{8,12},{12,16},{16,20},{20,24},{24,28},{1,5},{5,9},{9,... | collective-permute-start | bytes 196616 | tf_op jit(solution)/shard_map/ppermute | solution.py:17
  246.9 5.9 %collective-permute-start.18 = (f32[2,4,10,1,128]{4,3,2,1,0:T(1,128)S(1)}, f32[2,4,10,1,128]{4,3,2,1,0:T(1,128)S(1)}, u32[]{:S(2)}, u32[]{:S(2)}) collective-permute-start(f32[2,4,10,1,128]{4,3,2,1,0:T(1,128)S(1)} %get-tuple-element.45), channel_id=1, source_target_pairs={{1,0},{2,1},{3,2},{5,4},{6,5},{7,6},{9,8},{10,9},{11,10},{13,12},{... | collective-permute-start | bytes 122888 | tf_op jit(solution)/shard_map/ppermute | solution.py:18
  248.8 5.9 %collective-permute-start.19 = (f32[2,4,10,1,128]{4,3,2,1,0:T(1,128)S(1)}, f32[2,4,10,1,128]{4,3,2,1,0:T(1,128)S(1)}, u32[]{:S(2)}, u32[]{:S(2)}) collective-permute-start(f32[2,4,10,1,128]{4,3,2,1,0:T(1,128)S(1)} %get-tuple-element.46), channel_id=1, source_target_pairs={{0,1},{1,2},{2,3},{4,5},{5,6},{6,7},{8,9},{9,10},{10,11},{12,13},{... | collective-permute-start | bytes 122888 | tf_op jit(solution)/shard_map/ppermute | solution.py:17
  256.0 7.8 %collective-permute-start.20 = (f32[2,4,1,16,128]{4,3,2,1,0:T(8,128)S(1)}, f32[2,4,1,16,128]{4,3,2,1,0:T(8,128)S(1)}, u32[]{:S(2)}, u32[]{:S(2)}) collective-permute-start(f32[2,4,1,16,128]{4,3,2,1,0:T(8,128)S(1)} %get-tuple-element.68), channel_id=1, source_target_pairs={{4,0},{8,4},{12,8},{16,12},{20,16},{24,20},{28,24},{5,1},{9,5},{13... | collective-permute-start | bytes 196616 | tf_op jit(solution)/shard_map/ppermute | solution.py:18
  257.3 7.7 %collective-permute-start.21 = (f32[2,4,1,16,128]{4,3,2,1,0:T(8,128)S(1)}, f32[2,4,1,16,128]{4,3,2,1,0:T(8,128)S(1)}, u32[]{:S(2)}, u32[]{:S(2)}) collective-permute-start(f32[2,4,1,16,128]{4,3,2,1,0:T(8,128)S(1)} %get-tuple-element.67), channel_id=1, source_target_pairs={{0,4},{4,8},{8,12},{12,16},{16,20},{20,24},{24,28},{1,5},{5,9},{9,... | collective-permute-start | bytes 196616 | tf_op jit(solution)/shard_map/ppermute | solution.py:17
  265.1 5.9 %collective-permute-start.22 = (f32[2,4,10,1,128]{4,3,2,1,0:T(1,128)S(1)}, f32[2,4,10,1,128]{4,3,2,1,0:T(1,128)S(1)}, u32[]{:S(2)}, u32[]{:S(2)}) collective-permute-start(f32[2,4,10,1,128]{4,3,2,1,0:T(1,128)S(1)} %get-tuple-element.43), channel_id=1, source_target_pairs={{1,0},{2,1},{3,2},{5,4},{6,5},{7,6},{9,8},{10,9},{11,10},{13,12},{... | collective-permute-start | bytes 122888 | tf_op jit(solution)/shard_map/ppermute | solution.py:18
  267.0 5.9 %collective-permute-start.23 = (f32[2,4,10,1,128]{4,3,2,1,0:T(1,128)S(1)}, f32[2,4,10,1,128]{4,3,2,1,0:T(1,128)S(1)}, u32[]{:S(2)}, u32[]{:S(2)}) collective-permute-start(f32[2,4,10,1,128]{4,3,2,1,0:T(1,128)S(1)} %get-tuple-element.44), channel_id=1, source_target_pairs={{0,1},{1,2},{2,3},{4,5},{5,6},{6,7},{8,9},{9,10},{10,11},{12,13},{... | collective-permute-start | bytes 122888 | tf_op jit(solution)/shard_map/ppermute | solution.py:17
  274.8 31.4 %collective-permute-start.24 = (f32[2,4,1,16,128]{4,3,2,1,0:T(8,128)}, f32[2,4,1,16,128]{4,3,2,1,0:T(8,128)S(1)}, u32[]{:S(2)}, u32[]{:S(2)}) collective-permute-start(f32[2,4,1,16,128]{4,3,2,1,0:T(8,128)} %get-tuple-element.66), channel_id=1, source_target_pairs={{4,0},{8,4},{12,8},{16,12},{20,16},{24,20},{28,24},{5,1},{9,5},{13... | collective-permute-start | bytes 196616 | tf_op jit(solution)/shard_map/ppermute | solution.py:18
  276.0 30.1 %collective-permute-start.25 = (f32[2,4,1,16,128]{4,3,2,1,0:T(8,128)}, f32[2,4,1,16,128]{4,3,2,1,0:T(8,128)S(1)}, u32[]{:S(2)}, u32[]{:S(2)}) collective-permute-start(f32[2,4,1,16,128]{4,3,2,1,0:T(8,128)} %get-tuple-element.65), channel_id=1, source_target_pairs={{0,4},{4,8},{8,12},{12,16},{16,20},{20,24},{24,28},{1,5},{5,9},{9,... | collective-permute-start | bytes 196616 | tf_op jit(solution)/shard_map/ppermute | solution.py:17
  306.2 6.0 %collective-permute-start.26 = (f32[2,4,10,1,128]{4,3,2,1,0:T(1,128)S(1)}, f32[2,4,10,1,128]{4,3,2,1,0:T(1,128)S(1)}, u32[]{:S(2)}, u32[]{:S(2)}) collective-permute-start(f32[2,4,10,1,128]{4,3,2,1,0:T(1,128)S(1)} %get-tuple-element.41), channel_id=1, source_target_pairs={{1,0},{2,1},{3,2},{5,4},{6,5},{7,6},{9,8},{10,9},{11,10},{13,12},{... | collective-permute-start | bytes 122888 | tf_op jit(solution)/shard_map/ppermute | solution.py:18
  308.2 5.9 %collective-permute-start.27 = (f32[2,4,10,1,128]{4,3,2,1,0:T(1,128)S(1)}, f32[2,4,10,1,128]{4,3,2,1,0:T(1,128)S(1)}, u32[]{:S(2)}, u32[]{:S(2)}) collective-permute-start(f32[2,4,10,1,128]{4,3,2,1,0:T(1,128)S(1)} %get-tuple-element.42), channel_id=1, source_target_pairs={{0,1},{1,2},{2,3},{4,5},{5,6},{6,7},{8,9},{9,10},{10,11},{12,13},{... | collective-permute-start | bytes 122888 | tf_op jit(solution)/shard_map/ppermute | solution.py:17
  315.3 10.1 %collective-permute-start.28 = (f32[2,4,1,16,128]{4,3,2,1,0:T(8,128)S(1)}, f32[2,4,1,16,128]{4,3,2,1,0:T(8,128)S(1)}, u32[]{:S(2)}, u32[]{:S(2)}) collective-permute-start(f32[2,4,1,16,128]{4,3,2,1,0:T(8,128)S(1)} %get-tuple-element.64), channel_id=1, source_target_pairs={{4,0},{8,4},{12,8},{16,12},{20,16},{24,20},{28,24},{5,1},{9,5},{13... | collective-permute-start | bytes 196616 | tf_op jit(solution)/shard_map/ppermute | solution.py:18
  316.7 8.6 %collective-permute-start.29 = (f32[2,4,1,16,128]{4,3,2,1,0:T(8,128)S(1)}, f32[2,4,1,16,128]{4,3,2,1,0:T(8,128)S(1)}, u32[]{:S(2)}, u32[]{:S(2)}) collective-permute-start(f32[2,4,1,16,128]{4,3,2,1,0:T(8,128)S(1)} %get-tuple-element.63), channel_id=1, source_target_pairs={{0,4},{4,8},{8,12},{12,16},{16,20},{20,24},{24,28},{1,5},{5,9},{9,... | collective-permute-start | bytes 196616 | tf_op jit(solution)/shard_map/ppermute | solution.py:17
  325.5 6.0 %collective-permute-start.30 = (f32[2,4,10,1,128]{4,3,2,1,0:T(1,128)S(1)}, f32[2,4,10,1,128]{4,3,2,1,0:T(1,128)S(1)}, u32[]{:S(2)}, u32[]{:S(2)}) collective-permute-start(f32[2,4,10,1,128]{4,3,2,1,0:T(1,128)S(1)} %get-tuple-element.39), channel_id=1, source_target_pairs={{1,0},{2,1},{3,2},{5,4},{6,5},{7,6},{9,8},{10,9},{11,10},{13,12},{... | collective-permute-start | bytes 122888 | tf_op jit(solution)/shard_map/ppermute | solution.py:18
  327.4 5.9 %collective-permute-start.31 = (f32[2,4,10,1,128]{4,3,2,1,0:T(1,128)S(1)}, f32[2,4,10,1,128]{4,3,2,1,0:T(1,128)S(1)}, u32[]{:S(2)}, u32[]{:S(2)}) collective-permute-start(f32[2,4,10,1,128]{4,3,2,1,0:T(1,128)S(1)} %get-tuple-element.40), channel_id=1, source_target_pairs={{0,1},{1,2},{2,3},{4,5},{5,6},{6,7},{8,9},{9,10},{10,11},{12,13},{... | collective-permute-start | bytes 122888 | tf_op jit(solution)/shard_map/ppermute | solution.py:17
  334.0 7.2 %collective-permute-start.32 = (f32[2,4,1,16,128]{4,3,2,1,0:T(8,128)S(1)}, f32[2,4,1,16,128]{4,3,2,1,0:T(8,128)S(1)}, u32[]{:S(2)}, u32[]{:S(2)}) collective-permute-start(f32[2,4,1,16,128]{4,3,2,1,0:T(8,128)S(1)} %get-tuple-element.62), channel_id=1, source_target_pairs={{4,0},{8,4},{12,8},{16,12},{20,16},{24,20},{28,24},{5,1},{9,5},{13... | collective-permute-start | bytes 196616 | tf_op jit(solution)/shard_map/ppermute | solution.py:18
  335.4 7.3 %collective-permute-start.33 = (f32[2,4,1,16,128]{4,3,2,1,0:T(8,128)S(1)}, f32[2,4,1,16,128]{4,3,2,1,0:T(8,128)S(1)}, u32[]{:S(2)}, u32[]{:S(2)}) collective-permute-start(f32[2,4,1,16,128]{4,3,2,1,0:T(8,128)S(1)} %get-tuple-element.61), channel_id=1, source_target_pairs={{0,4},{4,8},{8,12},{12,16},{16,20},{20,24},{24,28},{1,5},{5,9},{9,... | collective-permute-start | bytes 196616 | tf_op jit(solution)/shard_map/ppermute | solution.py:17
  342.8 6.1 %collective-permute-start.34 = (f32[2,4,10,1,128]{4,3,2,1,0:T(1,128)S(1)}, f32[2,4,10,1,128]{4,3,2,1,0:T(1,128)S(1)}, u32[]{:S(2)}, u32[]{:S(2)}) collective-permute-start(f32[2,4,10,1,128]{4,3,2,1,0:T(1,128)S(1)} %get-tuple-element.37), channel_id=1, source_target_pairs={{1,0},{2,1},{3,2},{5,4},{6,5},{7,6},{9,8},{10,9},{11,10},{13,12},{... | collective-permute-start | bytes 122888 | tf_op jit(solution)/shard_map/ppermute | solution.py:18
  344.8 9.0 %collective-permute-start.35 = (f32[2,4,10,1,128]{4,3,2,1,0:T(1,128)S(1)}, f32[2,4,10,1,128]{4,3,2,1,0:T(1,128)S(1)}, u32[]{:S(2)}, u32[]{:S(2)}) collective-permute-start(f32[2,4,10,1,128]{4,3,2,1,0:T(1,128)S(1)} %get-tuple-element.38), channel_id=1, source_target_pairs={{0,1},{1,2},{2,3},{4,5},{5,6},{6,7},{8,9},{9,10},{10,11},{12,13},{... | collective-permute-start | bytes 122888 | tf_op jit(solution)/shard_map/ppermute | solution.py:17
  348.9 32.0 %collective-permute-start.53 = (f32[1,16,128]{2,1,0:T(8,128)S(1)}, f32[1,16,128]{2,1,0:T(8,128)S(1)}, u32[]{:S(2)}, u32[]{:S(2)}) collective-permute-start(f32[1,16,128]{2,1,0:T(8,128)S(1)} %copy-done.73), channel_id=1, source_target_pairs={{0,4},{4,8},{8,12},{12,16},{16,20},{20,24},{24,28},{1,5},{5,9},{9,... | collective-permute-start | bytes 24584 | tf_op jit(solution)/shard_map/ppermute | solution.py:17
  353.8 47.3 %collective-permute-start.56 = (f32[1,16,128]{2,1,0:T(8,128)S(1)}, f32[1,16,128]{2,1,0:T(8,128)S(1)}, u32[]{:S(2)}, u32[]{:S(2)}) collective-permute-start(f32[1,16,128]{2,1,0:T(8,128)S(1)} %copy-done.75), channel_id=1, source_target_pairs={{4,0},{8,4},{12,8},{16,12},{20,16},{24,20},{28,24},{5,1},{9,5},{13... | collective-permute-start | bytes 24584 | tf_op jit(solution)/shard_map/ppermute | solution.py:18
  356.5 8.5 %collective-permute-start.36 = (f32[2,4,1,16,128]{4,3,2,1,0:T(8,128)S(1)}, f32[2,4,1,16,128]{4,3,2,1,0:T(8,128)S(1)}, u32[]{:S(2)}, u32[]{:S(2)}) collective-permute-start(f32[2,4,1,16,128]{4,3,2,1,0:T(8,128)S(1)} %get-tuple-element.60), channel_id=1, source_target_pairs={{4,0},{8,4},{12,8},{16,12},{20,16},{24,20},{28,24},{5,1},{9,5},{13... | collective-permute-start | bytes 196616 | tf_op jit(solution)/shard_map/ppermute | solution.py:18
  357.8 8.3 %collective-permute-start.37 = (f32[2,4,1,16,128]{4,3,2,1,0:T(8,128)S(1)}, f32[2,4,1,16,128]{4,3,2,1,0:T(8,128)S(1)}, u32[]{:S(2)}, u32[]{:S(2)}) collective-permute-start(f32[2,4,1,16,128]{4,3,2,1,0:T(8,128)S(1)} %get-tuple-element.59), channel_id=1, source_target_pairs={{0,4},{4,8},{8,12},{12,16},{16,20},{20,24},{24,28},{1,5},{5,9},{9,... | collective-permute-start | bytes 196616 | tf_op jit(solution)/shard_map/ppermute | solution.py:17
  366.2 5.9 %collective-permute-start.38 = (f32[2,4,10,1,128]{4,3,2,1,0:T(1,128)S(1)}, f32[2,4,10,1,128]{4,3,2,1,0:T(1,128)S(1)}, u32[]{:S(2)}, u32[]{:S(2)}) collective-permute-start(f32[2,4,10,1,128]{4,3,2,1,0:T(1,128)S(1)} %get-tuple-element.35), channel_id=1, source_target_pairs={{1,0},{2,1},{3,2},{5,4},{6,5},{7,6},{9,8},{10,9},{11,10},{13,12},{... | collective-permute-start | bytes 122888 | tf_op jit(solution)/shard_map/ppermute | solution.py:18
  368.1 8.8 %collective-permute-start.39 = (f32[2,4,10,1,128]{4,3,2,1,0:T(1,128)S(1)}, f32[2,4,10,1,128]{4,3,2,1,0:T(1,128)S(1)}, u32[]{:S(2)}, u32[]{:S(2)}) collective-permute-start(f32[2,4,10,1,128]{4,3,2,1,0:T(1,128)S(1)} %get-tuple-element.36), channel_id=1, source_target_pairs={{0,1},{1,2},{2,3},{4,5},{5,6},{6,7},{8,9},{9,10},{10,11},{12,13},{... | collective-permute-start | bytes 122888 | tf_op jit(solution)/shard_map/ppermute | solution.py:17
  372.1 30.2 %collective-permute-start.57 = (f32[1,16,128]{2,1,0:T(8,128)S(1)}, f32[1,16,128]{2,1,0:T(8,128)S(1)}, u32[]{:S(2)}, u32[]{:S(2)}) collective-permute-start(f32[1,16,128]{2,1,0:T(8,128)S(1)} %copy-done.74), channel_id=1, source_target_pairs={{0,4},{4,8},{8,12},{12,16},{16,20},{20,24},{24,28},{1,5},{5,9},{9,... | collective-permute-start | bytes 24584 | tf_op jit(solution)/shard_map/ppermute | solution.py:17
  377.0 47.2 %collective-permute-start.50 = (f32[10,1,128]{2,1,0:T(1,128)S(1)}, f32[10,1,128]{2,1,0:T(1,128)S(1)}, u32[]{:S(2)}, u32[]{:S(2)}) collective-permute-start(f32[10,1,128]{2,1,0:T(1,128)S(1)} %get-tuple-element.91), channel_id=1, source_target_pairs={{1,0},{2,1},{3,2},{5,4},{6,5},{7,6},{9,8},{10,9},{11,10},{13,12},{... | collective-permute-start | bytes 15368 | tf_op jit(solution)/shard_map/ppermute | solution.py:18
  379.6 7.8 %collective-permute-start.40 = (f32[2,4,1,16,128]{4,3,2,1,0:T(8,128)S(1)}, f32[2,4,1,16,128]{4,3,2,1,0:T(8,128)S(1)}, u32[]{:S(2)}, u32[]{:S(2)}) collective-permute-start(f32[2,4,1,16,128]{4,3,2,1,0:T(8,128)S(1)} %get-tuple-element.58), channel_id=1, source_target_pairs={{4,0},{8,4},{12,8},{16,12},{20,16},{24,20},{28,24},{5,1},{9,5},{13... | collective-permute-start | bytes 196616 | tf_op jit(solution)/shard_map/ppermute | solution.py:18
  380.9 7.7 %collective-permute-start.41 = (f32[2,4,1,16,128]{4,3,2,1,0:T(8,128)S(1)}, f32[2,4,1,16,128]{4,3,2,1,0:T(8,128)S(1)}, u32[]{:S(2)}, u32[]{:S(2)}) collective-permute-start(f32[2,4,1,16,128]{4,3,2,1,0:T(8,128)S(1)} %get-tuple-element.57), channel_id=1, source_target_pairs={{0,4},{4,8},{8,12},{12,16},{16,20},{20,24},{24,28},{1,5},{5,9},{9,... | collective-permute-start | bytes 196616 | tf_op jit(solution)/shard_map/ppermute | solution.py:17
  388.6 5.9 %collective-permute-start.42 = (f32[2,4,10,1,128]{4,3,2,1,0:T(1,128)S(1)}, f32[2,4,10,1,128]{4,3,2,1,0:T(1,128)S(1)}, u32[]{:S(2)}, u32[]{:S(2)}) collective-permute-start(f32[2,4,10,1,128]{4,3,2,1,0:T(1,128)S(1)} %get-tuple-element.33), channel_id=1, source_target_pairs={{1,0},{2,1},{3,2},{5,4},{6,5},{7,6},{9,8},{10,9},{11,10},{13,12},{... | collective-permute-start | bytes 122888 | tf_op jit(solution)/shard_map/ppermute | solution.py:18
  390.6 7.9 %collective-permute-start.43 = (f32[2,4,10,1,128]{4,3,2,1,0:T(1,128)S(1)}, f32[2,4,10,1,128]{4,3,2,1,0:T(1,128)S(1)}, u32[]{:S(2)}, u32[]{:S(2)}) collective-permute-start(f32[2,4,10,1,128]{4,3,2,1,0:T(1,128)S(1)} %get-tuple-element.34), channel_id=1, source_target_pairs={{0,1},{1,2},{2,3},{4,5},{5,6},{6,7},{8,9},{9,10},{10,11},{12,13},{... | collective-permute-start | bytes 122888 | tf_op jit(solution)/shard_map/ppermute | solution.py:17
  394.5 33.6 %collective-permute-start.51 = (f32[10,1,128]{2,1,0:T(1,128)S(1)}, f32[10,1,128]{2,1,0:T(1,128)S(1)}, u32[]{:S(2)}, u32[]{:S(2)}) collective-permute-start(f32[10,1,128]{2,1,0:T(1,128)S(1)} %get-tuple-element.92), channel_id=1, source_target_pairs={{0,1},{1,2},{2,3},{4,5},{5,6},{6,7},{8,9},{9,10},{10,11},{12,13},{... | collective-permute-start | bytes 15368 | tf_op jit(solution)/shard_map/ppermute | solution.py:17
  398.5 29.7 %collective-permute-start.54 = (f32[10,1,128]{2,1,0:T(1,128)S(1)}, f32[10,1,128]{2,1,0:T(1,128)S(1)}, u32[]{:S(2)}, u32[]{:S(2)}) collective-permute-start(f32[10,1,128]{2,1,0:T(1,128)S(1)} %get-tuple-element.93), channel_id=1, source_target_pairs={{1,0},{2,1},{3,2},{5,4},{6,5},{7,6},{9,8},{10,9},{11,10},{13,12},{... | collective-permute-start | bytes 15368 | tf_op jit(solution)/shard_map/ppermute | solution.py:18
  401.1 7.1 %collective-permute-start.44 = (f32[2,4,1,16,128]{4,3,2,1,0:T(8,128)S(1)}, f32[2,4,1,16,128]{4,3,2,1,0:T(8,128)S(1)}, u32[]{:S(2)}, u32[]{:S(2)}) collective-permute-start(f32[2,4,1,16,128]{4,3,2,1,0:T(8,128)S(1)} %get-tuple-element.56), channel_id=1, source_target_pairs={{4,0},{8,4},{12,8},{16,12},{20,16},{24,20},{28,24},{5,1},{9,5},{13... | collective-permute-start | bytes 196616 | tf_op jit(solution)/shard_map/ppermute | solution.py:18
  402.4 7.4 %collective-permute-start.45 = (f32[2,4,1,16,128]{4,3,2,1,0:T(8,128)S(1)}, f32[2,4,1,16,128]{4,3,2,1,0:T(8,128)S(1)}, u32[]{:S(2)}, u32[]{:S(2)}) collective-permute-start(f32[2,4,1,16,128]{4,3,2,1,0:T(8,128)S(1)} %get-tuple-element.55), channel_id=1, source_target_pairs={{0,4},{4,8},{8,12},{12,16},{16,20},{20,24},{24,28},{1,5},{5,9},{9,... | collective-permute-start | bytes 196616 | tf_op jit(solution)/shard_map/ppermute | solution.py:17
  409.8 6.2 %collective-permute-start.46 = (f32[2,4,10,1,128]{4,3,2,1,0:T(1,128)S(1)}, f32[2,4,10,1,128]{4,3,2,1,0:T(1,128)S(1)}, u32[]{:S(2)}, u32[]{:S(2)}) collective-permute-start(f32[2,4,10,1,128]{4,3,2,1,0:T(1,128)S(1)} %get-tuple-element.31), channel_id=1, source_target_pairs={{1,0},{2,1},{3,2},{5,4},{6,5},{7,6},{9,8},{10,9},{11,10},{13,12},{... | collective-permute-start | bytes 122888 | tf_op jit(solution)/shard_map/ppermute | solution.py:18
  411.7 8.3 %collective-permute-start.47 = (f32[2,4,10,1,128]{4,3,2,1,0:T(1,128)S(1)}, f32[2,4,10,1,128]{4,3,2,1,0:T(1,128)S(1)}, u32[]{:S(2)}, u32[]{:S(2)}) collective-permute-start(f32[2,4,10,1,128]{4,3,2,1,0:T(1,128)S(1)} %get-tuple-element.32), channel_id=1, source_target_pairs={{0,1},{1,2},{2,3},{4,5},{5,6},{6,7},{8,9},{9,10},{10,11},{12,13},{... | collective-permute-start | bytes 122888 | tf_op jit(solution)/shard_map/ppermute | solution.py:17
  416.0 12.2 %collective-permute-start.55 = (f32[10,1,128]{2,1,0:T(1,128)S(1)}, f32[10,1,128]{2,1,0:T(1,128)S(1)}, u32[]{:S(2)}, u32[]{:S(2)}) collective-permute-start(f32[10,1,128]{2,1,0:T(1,128)S(1)} %get-tuple-element.94), channel_id=1, source_target_pairs={{0,1},{1,2},{2,3},{4,5},{5,6},{6,7},{8,9},{9,10},{10,11},{12,13},{... | collective-permute-start | bytes 15368 | tf_op jit(solution)/shard_map/ppermute | solution.py:17
  420.1 8.1 %collective-permute-start.58 = (f32[10,1,128]{2,1,0:T(1,128)S(1)}, f32[10,1,128]{2,1,0:T(1,128)S(1)}, u32[]{:S(2)}, u32[]{:S(2)}) collective-permute-start(f32[10,1,128]{2,1,0:T(1,128)S(1)} %get-tuple-element.95), channel_id=1, source_target_pairs={{1,0},{2,1},{3,2},{5,4},{6,5},{7,6},{9,8},{10,9},{11,10},{13,12},{... | collective-permute-start | bytes 15368 | tf_op jit(solution)/shard_map/ppermute | solution.py:18
  424.1 5.5 %collective-permute-start.59 = (f32[10,1,128]{2,1,0:T(1,128)S(1)}, f32[10,1,128]{2,1,0:T(1,128)S(1)}, u32[]{:S(2)}, u32[]{:S(2)}) collective-permute-start(f32[10,1,128]{2,1,0:T(1,128)S(1)} %get-tuple-element.96), channel_id=1, source_target_pairs={{0,1},{1,2},{2,3},{4,5},{5,6},{6,7},{8,9},{9,10},{10,11},{12,13},{... | collective-permute-start | bytes 15368 | tf_op jit(solution)/shard_map/ppermute | solution.py:17
  (80 other events, 1101.0 us)
Sparse Core Ops, SparseCore 0:
  431.8 43.7 reduce-scatter.3
